TPU v7x, 256 devices: a whole 4x4x8 slice. The times are simulated.
256 devices in a mesh: gx: 4 (over y), gy: 4 (over z_hi, core), gz: 16 (over x, z_lo).
Axes of the slice: x: 4, y: 4, z: 8 (z_hi: 2, z_lo: 4; z = z_hi * 4 + z_lo), core: 2. Of those that a mesh axis runs over, the one named last changes fastest.
Arguments:
- concentration: float32 [192, 64, 2048], P('gx', 'gy', 'gz'), may hold values from -6 to 6
- dispersion: float32 [192, 64, 2048], P('gx', 'gy', 'gz'), may hold values from 0.2 to 1.2
- disp_step: float32 [192, 64, 2048], P('gx', 'gy', 'gz'), may hold values from -6 to 6
- capacity: float32 [192, 64, 2048], P('gx', 'gy', 'gz'), may hold values from 1 to 4
- cap_step: float32 [192, 64, 2048], P('gx', 'gy', 'gz'), may hold values from -6 to 6
- velocity: float32 [192, 64, 2048], P('gx', 'gy', 'gz'), may hold values from 0.2 to 1
- voxel_mask: int32 [24, 8, 256], P('gx', 'gy', 'gz'), may hold values 0 or 1
- voxel_class: int32 [24, 8, 256], P('gx', 'gy', 'gz'), may hold values from 0 to 3
- class_weight: float32 [4], replicated, may hold values from 4 to 40
Outputs:
- grad_dispersion: float32 [192, 64, 2048], P('gx', 'gy', 'gz')
- grad_capacity: float32 [192, 64, 2048], P('gx', 'gy', 'gz')
All inputs are finite; a program needn't handle non-finite values. No bound on the sum of `voxel_mask` on one device may be relied on, other than what follows from the above.
Results may differ from a plain program's by a relative error of at most 0.00024.
Values sent between devices are 32-bit elements; how exact they have to be, the bound alone decides.
No kernel may reach another device: no remote copies, remote signals or barrier semaphores. Data moves between devices by JAX's collectives and lax.ppermute only.
A program may use at most 64 MiB of HBM per device.

v0:
```python
from functools import partial

import jax
import jax.numpy as jnp
from jax import lax
from jax.experimental import pallas as pl
from jax.experimental.pallas import tpu as pltpu
from jax.sharding import PartitionSpec as P


DT = 0.1
U1, U2, U3, U4 = (5, 4, 10, 8)
F32 = jnp.float32
VM = pl.BlockSpec(memory_space=pltpu.VMEM)
SM = pl.BlockSpec(memory_space=pltpu.SMEM)
HB = pl.BlockSpec(memory_space=pltpu.HBM)


def swap_pairs(size, first):
    pairs = []
    for i in range(first, size, 2):
        pairs += [(i, (i + 1) % size), ((i + 1) % size, i)]
    return pairs


def swap(value, axis, first):
    return lax.ppermute(value, axis, swap_pairs(lax.axis_size(axis), first))


def call(body, outs, specs, args, scratch=(), limit=24, alias=None):
    return pl.pallas_call(
        body,
        out_shape=[jax.ShapeDtypeStruct(s, F32) for s in outs],
        in_specs=specs,
        out_specs=[VM] * len(outs),
        scratch_shapes=list(scratch),
        input_output_aliases=alias or {},
        compiler_params=pltpu.CompilerParams(vmem_limit_bytes=limit << 20),
    )(*args)


def rows(shape):
    return lax.broadcasted_iota(jnp.int32, shape, len(shape) - 2)


def lanes(shape):
    return lax.broadcasted_iota(jnp.int32, shape, len(shape) - 1)


def up(x, axis):
    return pltpu.roll(x, x.shape[axis] - 1, axis)


def down(x, axis):
    return pltpu.roll(x, 1, axis)


def rolled(x, shift, axis):
    shift = shift % x.shape[axis]
    return x if shift == 0 else pltpu.roll(x, shift, axis)


def is_even(idx, axis):
    return idx[axis] % 2 == 0


def picked(ends, idx, axis, r0, r1):
    even = is_even(idx, axis)
    lo = jnp.where(even, r1, r0)
    hi = jnp.where(even, r0, r1)
    return jnp.where(idx[axis] > 0, lo, 0.0), jnp.where(idx[axis] < ends[axis], hi, 0.0)


def pack_a(idx, c, d, s, cap, m, v, all_f, bx0, bx1, by0, by1, ys0, ys1, sems):
    n = c.shape[0]
    xeven = is_even(idx, 0)
    yeven = is_even(idx, 1)
    row = rows((8, 128))
    copies = [
        pltpu.make_async_copy(ref, all_f.at[f], sems.at[f])
        for f, ref in enumerate((c, d, s, cap, m, v))
    ]
    for copy in copies:
        copy.start()
    for copy in copies:
        copy.wait()
    for out, hi in ((bx0, xeven), (bx1, jnp.logical_not(xeven))):
        one = jnp.where(hi, n - 1, 0)
        two = jnp.where(hi, n - 2, 1)
        for slot, (f, at) in enumerate(
            [(f, i) for f in range(4) for i in (one, two)] + [(4, one), (5, one)]
        ):
            out[slot] = all_f[f, at]

    def tiles(four, low):
        out = None
        for f, value in enumerate(four):
            part = rolled(value, 2 * f if low else 2 * f + 2, 0)
            out = part if f == 0 else jnp.where(row < 2 * f, out, part)
        return out

    def put(at, lo, hi):
        by0[at] = jnp.where(yeven, hi, lo)
        by1[at] = jnp.where(yeven, lo, hi)

    def group(g, _):
        lo = hi = None
        for k in range(8):
            x = g * 4 + k // 2
            if k % 2 == 0:
                put(
                    x,
                    tiles([all_f[f, x, 0:8, :] for f in range(4)], True),
                    tiles([all_f[f, x, 8:16, :] for f in range(4)], False),
                )
            a = rolled(all_f[4 + k % 2, x, 0:8, :], k, 0)
            b = rolled(all_f[4 + k % 2, x, 8:16, :], k + 1, 0)
            lo = a if k == 0 else jnp.where(row < k, lo, a)
            hi = b if k == 0 else jnp.where(row < k, hi, b)
        put(n + g, lo, hi)
        return 0

    lax.fori_loop(0, n // 4, group, 0, unroll=2)
    lane = lanes((8, 128))
    for ys in (ys0, ys1):
        ys[0:4] = jnp.zeros((4, 8, 128), F32)
    for ys, by in ((ys0, by0), (ys1, by1)):
        ys[4] = by[0]
        ys[5] = by[n - 1]

    def ends_of(g, _):
        out = [None] * 4
        for k in range(8):
            x = g * 8 + k
            parts = (by0[x], by1[x], all_f[5, x, 0:8, :], all_f[5, x, 8:16, :])
            for i, value in enumerate(parts):
                part = rolled(value, 4 * k + 2, 1)
                out[i] = part if k == 0 else jnp.where(lane < 4 * k, out[i], part)
        at = g * 32 + 8
        for col in range(2):
            shift = (at - 128 * col) & 127
            here = (lane + 128 * col >= at) & (lane + 128 * col < at + 32)
            one, two, low, high = (pltpu.roll(q, shift, 1) for q in out)
            v0 = jnp.where(yeven, high, low)
            v1 = jnp.where(yeven, low, high)
            for ys, i, value in ((ys0, 0, one), (ys1, 0, two), (ys0, 2, v0), (ys1, 2, v1)):
                ys[i + col] = jnp.where(here, value, ys[i + col])
        return 0

    lax.fori_loop(0, n // 8, ends_of, 0, unroll=2)


def pack_t(all_f, t):
    n = all_f.shape[1]
    lane = lanes((16, 128))
    t[...] = jnp.zeros(t.shape, F32)

    def pack(g, _):
        at = g * 32 + 8
        for f in range(6):
            out = None
            for k in range(8):
                part = rolled(all_f[f, g * 8 + k], 4 * k + 2, 1)
                out = part if k == 0 else jnp.where(lane < 4 * k, out, part)
            out = pltpu.roll(out, at & 127, 1)
            for col in range(2):
                here = (lane + 128 * col >= at) & (lane + 128 * col < at + 32)
                t[f, col] = jnp.where(here, out, t[f, col])
        return 0

    lax.fori_loop(0, n // 8, pack, 0)


def third(hi, lo, f):
    row = rows((8, 128))
    return jnp.where(row < 4, rolled(hi, -2 * f, 0), rolled(lo, 6 - 2 * f, 0))


def pack_b(ends, planes, idx, tm, rx0, rx1, ys0, ys1, t, e0, e1):
    xeven = is_even(idx, 0)
    row = rows((8, 128))
    lane = lanes((16, 128))
    tiles = [picked(ends, idx, 1, ys0[k], ys1[k]) for k in range(6)]
    for f in range(6):
        halo = picked(ends, idx, 0, rx0[2 * f if f < 4 else 4 + f], rx1[2 * f if f < 4 else 4 + f])
        for col in range(2):
            at = (1, planes + 2)[col]
            part = rolled(halo[col], 4 * at + 2, 1)
            t[f, col, 0:16, :] = jnp.where(lane // 4 == at % 32, part, tm[f, col])
            if f < 4:
                t[f, col, 16:24, :] = third(tiles[col][1], tiles[col][0], f)
            elif f == 4:
                t[f, col, 16:24, :] = jnp.zeros((8, 128), F32)
            else:
                t[f, col, 16:24, :] = jnp.where(row < 4, tiles[2 + col][1], tiles[2 + col][0])
    for f in range(4):
        lo, hi = (third(tiles[k][1], tiles[k][0], f) for k in (4, 5))
        e0[f] = jnp.where(xeven, hi, lo)
        e1[f] = jnp.where(xeven, lo, hi)


def pack_c(ends, idx, all_f, rx0, rx1, ry0, ry1, p):
    n = all_f.shape[1]
    row = rows((8, 128))
    zero = jnp.zeros((8, 128), F32)

    def both(at):
        return picked(ends, idx, 1, ry0[at], ry1[at])

    def group(g, _):
        mvlo, mvhi = both(n + g)
        for k in range(4):
            x = g * 4 + k
            lo, hi = both(x)
            for f in range(6):
                p[f, x + 2, 0:16, :] = all_f[f, x]
                if f < 4:
                    p[f, x + 2, 16:24, :] = third(hi, lo, f)
                else:
                    r = 2 * k + f - 4
                    a, b = (rolled(mvhi, -r, 0), rolled(mvlo, 7 - r, 0))
                    p[f, x + 2, 16:24, :] = jnp.where(row < 4, a, b)
        return 0

    lax.fori_loop(0, n // 4, group, 0)
    for f in range(6):
        slot = 2 * f if f < 4 else 4 + f
        p[f, 1, 0:16, :], p[f, n + 2, 0:16, :] = picked(ends, idx, 0, rx0[slot], rx1[slot])
        if f < 4:
            p[f, 0, 0:16, :], p[f, n + 3, 0:16, :] = picked(ends, idx, 0, rx0[slot + 1], rx1[slot + 1])
        else:
            p[f, 0, 0:16, :] = jnp.zeros((16, 128), F32)
            p[f, n + 3, 0:16, :] = jnp.zeros((16, 128), F32)
        for e in (0, 1, n + 2, n + 3):
            p[f, e, 16:24, :] = zero


def wide(ref):
    return jnp.concatenate([ref[0], ref[1]], axis=1)


def ends_up(own, halo, slot):
    return jnp.where(slot == 1, up(own, 1), up(halo, 1))


def ends_down(own, halo, slot):
    return jnp.where(slot == 2, down(own, 1), down(halo, 1))


def ends_flow(k, f):
    kc, ku, kd = k
    fc, fu, fd = f
    fx = (kc + rolled(kc, -4, 1)) * (rolled(fc, -4, 1) - fc)
    fy = (kc + up(kc, 0)) * (up(fc, 0) - fc)
    flux = (fx - rolled(fx, 4, 1)) + (fy - down(fy, 0))
    return flux + ((kc + ku) * (fu - fc) - (kc + kd) * (fc - fd))


def to_ends(store, at, value, slot):
    value = jnp.where(slot == 1, up(value, 1), down(value, 1))
    store[at, 0] = value[:, 0:128]
    store[at, 1] = value[:, 128:256]


def edge(store, at, e, height=24):
    return pltpu.roll(store[at, e >> 5, 0:height, :], (126 - 4 * (e & 31)) & 127, 1)


def back(value, first, lane):
    return jnp.where(lane == 0, first, down(value, 1))


def inverse(cap):
    return DT * jnp.where(cap > 0, 1.0 / jnp.where(cap > 0, cap, 1.0), 0.0)


def forward(
    ends, idx, cw, p_in, t, rz0, rz1, re0, re1, mask, cls,
    p, v_out, h, a_out, later, later_z, r1, r2, tang, q_s, m, cs,
):
    n = r2.shape[0]
    for f in range(4):
        p[f, 1, 16:24, :], p[f, n + 2, 16:24, :] = picked(ends, idx, 0, re0[f], re1[f])

    slot = lanes((24, 256)) % 4
    own, halo = ([], [])
    for f in range(6):
        for col in range(2):
            lo, hi = picked(ends, idx, 2, rz0[f, col], rz1[f, col])
            h[f, col] = jnp.where(slot[:, 0:128] < 2, lo, hi)
        own.append(wide(t.at[f]))
        halo.append(wide(h.at[f]))
    near = [
        (halo[f], ends_up(own[f], halo[f], slot), ends_down(own[f], halo[f], slot)) for f in (0, 1, 2)
    ]
    vel, vel_down = (halo[5], ends_down(own[5], halo[5], slot))
    az = inverse(halo[3])
    qz = (1 / DT) * az * halo[4]
    rate = 0.5 * ends_flow(near[1], near[0]) + (vel_down * near[0][2] - vel * near[0][0])
    lz = near[0][0] + az * rate
    tz = az * (0.5 * ends_flow(near[2], near[0]) - qz * rate)
    later_z[0] = lz[:, 0:128]
    later_z[1] = lz[:, 128:256]
    for at, value in enumerate((halo[0], halo[1], halo[2], halo[5], lz, tz)):
        to_ends(m, at, value, slot)

    def make(e, _):
        a_out[e] = inverse(p[3, e])
        return 0

    lax.fori_loop(0, n + 4, make, 0, unroll=4)
    lane = lanes((24, 128))

    def first(t, carry):
        c0, d0, s0, fd, fs = carry
        e = t + 1
        c1, d1, s1 = (p[0, e + 1], p[1, e + 1], p[2, e + 1])
        ch, dh, sh, vh = (edge(m, k, e) for k in range(4))
        gx = c1 - c0
        fdx = (d0 + d1) * gx
        fsx = (s0 + s1) * gx
        gy = up(c0, 0) - c0
        fdy = (d0 + up(d0, 0)) * gy
        fsy = (s0 + up(s0, 0)) * gy
        gz = jnp.where(lane == 127, ch, up(c0, 1)) - c0
        fdz = (d0 + jnp.where(lane == 127, dh, up(d0, 1))) * gz
        fsz = (s0 + jnp.where(lane == 127, sh, up(s0, 1))) * gz
        gl = c0 - ch
        vc = p[5, e] * c0
        rate = (fdx - fd) + (fdy - down(fdy, 0)) + (fdz - back(fdz, (d0 + dh) * gl, lane))
        rate = 0.5 * rate + (back(vc, vh * ch, lane) - vc)
        other = (fsx - fs) + (fsy - down(fsy, 0)) + (fsz - back(fsz, (s0 + sh) * gl, lane))
        a = a_out[e]
        q = (1 / DT) * a * p[4, e]
        later[t] = c0 + a * rate
        tang[t] = a * (0.5 * other - q * rate)
        q_s[t] = q[0:16]
        r1[t] = rate[0:16]
        return c1, d1, s1, fdx, fsx

    c0, d0, s0 = (p[0, 0], p[1, 0], p[2, 0])
    c1, d1, s1 = (p[0, 1], p[1, 1], p[2, 1])
    start = (c1, d1, s1, (d0 + d1) * (c1 - c0), (s0 + s1) * (c1 - c0))
    lax.fori_loop(0, n + 2, first, start, unroll=U1)
    lane = lane[0:16]

    def second(x, carry):
        f1, f2, acc = carry
        t = x + 1
        e = t + 1
        l3, t3, d3, s3 = (later[t], tang[t], p[1, e], p[2, e])
        l0, t0, d0, s0 = (q[0:16] for q in (l3, t3, d3, s3))
        gl = later[t + 1, 0:16, :] - l0
        gt = tang[t + 1, 0:16, :] - t0
        dd = d0 + p[1, e + 1, 0:16, :]
        ss = s0 + p[2, e + 1, 0:16, :]
        fl = dd * gl
        ft = dd * gt + ss * gl
        dd = d3 + up(d3, 0)
        gly = up(l3, 0) - l3
        fly = dd * gly
        fty = dd * (up(t3, 0) - t3) + (s3 + up(s3, 0)) * gly
        dh, sh, vh, lh, th = (edge(m, k, e, 16) for k in (1, 2, 3, 4, 5))
        gl = jnp.where(lane == 127, lh, up(l0, 1)) - l0
        gt = jnp.where(lane == 127, th, up(t0, 1)) - t0
        dd = d0 + jnp.where(lane == 127, dh, up(d0, 1))
        ss = s0 + jnp.where(lane == 127, sh, up(s0, 1))
        flz = dd * gl
        ftz = dd * gt + ss * gl
        dd = d0 + dh
        gl = l0 - lh
        flb = back(flz, dd * gl, lane)
        ftb = back(ftz, dd * (t0 - th) + (s0 + sh) * gl, lane)
        vel = p[5, e, 0:16, :]
        vl = vel * l0
        vt = vel * t0
        rate = (fl - f1) + (fly - down(fly, 0))[0:16] + (flz - flb)
        rate = 0.5 * rate + (back(vl, vh * lh, lane) - vl)
        other = (ft - f2) + (fty - down(fty, 0))[0:16] + (ftz - ftb)
        other = 0.5 * other + (back(vt, vh * th, lane) - vt)
        final = t0 + a_out[e, 0:16, :] * (other - q_s[t] * rate)
        r2[x] = rate
        acc = jnp.where(x & 7 == 0, 0.0, acc) + final
        cs[x >> 3] = acc
        return fl, ft, acc

    gl = later[1, 0:16, :] - later[0, 0:16, :]
    gt = tang[1, 0:16, :] - tang[0, 0:16, :]
    dd = p[1, 1, 0:16, :] + p[1, 2, 0:16, :]
    ss = p[2, 1, 0:16, :] + p[2, 2, 0:16, :]
    lax.fori_loop(0, n, second, (dd * gl, dd * gt + ss * gl, jnp.zeros((16, 128), F32)), unroll=U2)

    lane8 = lanes((8, 128))
    row8 = rows((8, 128))
    expand = (
        lanes((16, 128)) // 8 == rows((16, 128))
    ).astype(F32)
    for yv in range(2):
        out = jnp.zeros((8, 128), F32)
        for X in range(n // 8):
            q = cs[X, 8 * yv : 8 * yv + 8, :]
            for k in (1, 2, 4):
                q = q + pltpu.roll(q, k, 0)
            for k in (1, 2, 4):
                q = q + jnp.where(lane8 & k == 0, pltpu.roll(q, 128 - k, 1), pltpu.roll(q, k, 1))
            out = jnp.where(row8 == X + 1, q, out)
        kind = cls[yv]
        weight = jnp.zeros(kind.shape, F32)
        for k in range(cw.shape[0]):
            weight = jnp.where(kind == k, cw[k], weight)
        weight = weight * mask[yv].astype(F32)
        spread = jnp.dot(weight, expand, precision=lax.Precision.HIGHEST, preferred_element_type=F32)
        v_out[yv] = out * spread * (1.0 / 512.0)


def merge(ends, idx, own, rx0, rx1, ry0, ry1, out, edge):
    row = rows((8, 128))
    for yv in range(2):
        lo, hi = picked(ends, idx, 0, rx0[yv], rx1[yv])
        value = jnp.where(row == 0, pltpu.roll(lo, 2, 0), own[yv])
        out[yv + 1] = jnp.where(row == 7, pltpu.roll(hi, 6, 0), value)
    lo = picked(ends, idx, 1, ry0[1], ry1[1])[0]
    hi = picked(ends, idx, 1, ry0[0], ry1[0])[1]
    for k, value in ((0, lo), (1, hi)):
        out[3 * k] = value
        edge[k] = value


def adjoint(
    ends, idx, vox, rz0, rz1, re0, re1, p, t, h, a_in, later, later_z, r1, r2,
    gd, gc, src, sc, sf, m,
):
    n = r2.shape[0]
    last = n // 8 + 1
    row = rows((8, 128))
    for X in range(last + 1):
        parts = []
        for yv in range(4):
            if X in (0, last) and yv in (0, 3):
                at, k = (last - 1 if X == 0 else 1, yv // 3)
                value = picked(ends, idx, 0, re0[k, at : at + 1, :], re1[k, at : at + 1, :])[X > 0]
            else:
                value = vox[yv, X : X + 1, :]
            parts.append(jnp.broadcast_to(value, (8, 128)))
        src[X, 0:8, :] = parts[1]
        src[X, 8:16, :] = parts[2]
        src[X, 16:24, :] = jnp.where(row < 4, parts[3], parts[0])

    slot8 = lanes((8, 128)) % 4
    sources = []
    for halo in (False, True):
        cols = []
        for col in range(2):
            here = (lanes((8, 128)) // 4 + 32 * col + 6) // 8 == row
            parts = []
            for yv in range(4):
                lo, hi = picked(ends, idx, 2, rz0[yv], rz1[yv]) if halo else (vox[yv], vox[yv])
                lo = jnp.broadcast_to(lo[:, 127:128], (8, 128))
                hi = jnp.broadcast_to(hi[:, 0:1], (8, 128))
                both = jnp.where(here, jnp.where(slot8 < 2, lo, hi), 0.0)
                for k in (1, 2, 4):
                    both = both + pltpu.roll(both, k, 0)
                parts.append(both)
            cols.append(
                jnp.concatenate([parts[1], parts[2], jnp.where(row < 4, parts[3], parts[0])], axis=0)
            )
        sources.append(jnp.concatenate(cols, axis=1))

    slot = lanes((24, 256)) % 4
    at, ah = (inverse(wide(t.at[3])), inverse(wide(h.at[3])))
    st, sh = (at * sources[0], ah * sources[1])
    dt, dh = (wide(t.at[1]), wide(h.at[1]))
    su = ends_up(st, sh, slot)
    flow = ends_flow(
        (dh, ends_up(dt, dh, slot), ends_down(dt, dh, slot)), (sh, su, ends_down(st, sh, slot))
    )
    fz = ah * (sources[1] + 0.5 * flow + wide(h.at[5]) * (su - sh))
    for k, value in enumerate((wide(h.at[0]), dh, sh, fz, wide(later_z))):
        to_ends(m, k, value, slot)

    def scale(e, _):
        sc[e] = a_in[e] * src[(e + 6) >> 3]
        return 0

    lax.fori_loop(0, n + 4, scale, 0, unroll=4)
    lane = lanes((24, 128))

    def third(t, f0):
        e = t + 1
        m0, d0 = (sc[e], p[1, e])
        dh, mh = (edge(m, 1, e), edge(m, 2, e))
        fx = (d0 + p[1, e + 1]) * (sc[e + 1] - m0)
        fy = (d0 + up(d0, 0)) * (up(m0, 0) - m0)
        gz = jnp.where(lane == 127, mh, up(m0, 1)) - m0
        fz = (d0 + jnp.where(lane == 127, dh, up(d0, 1))) * gz
        flow = (fx - f0) + (fy - down(fy, 0)) + (fz - back(fz, (d0 + dh) * (m0 - mh), lane))
        sf[t] = a_in[e] * (src[(e + 6) >> 3] + 0.5 * flow + p[5, e] * gz)
        return fx

    lax.fori_loop(0, n + 2, third, (p[1, 0] + p[1, 1]) * (sc[1] - sc[0]), unroll=U3)
    lane = lane[0:16]

    def fourth(x, e0):
        t = x + 1
        e = t + 1
        full = (sc[e], later[t], sf[t], p[0, e])
        m0, l0, s0, c0 = (q[0:16] for q in full)
        ex = (m0 - sc[e + 1, 0:16, :]) * (later[t + 1, 0:16, :] - l0)
        ex = ex + (s0 - sf[t + 1, 0:16, :]) * (p[0, e + 1, 0:16, :] - c0)
        m3, l3, s3, c3 = full
        ey = (m3 - up(m3, 0)) * (up(l3, 0) - l3) + (s3 - up(s3, 0)) * (up(c3, 0) - c3)
        ch, mh, sh, lh = (edge(m, k, e, 16) for k in (0, 2, 3, 4))
        mu, lu, su, cu = (
            jnp.where(lane == 127, b, up(a, 1)) for a, b in ((m0, mh), (l0, lh), (s0, sh), (c0, ch))
        )
        ez = (m0 - mu) * (lu - l0) + (s0 - su) * (cu - c0)
        eb = back(ez, (mh - m0) * (l0 - lh) + (sh - s0) * (c0 - ch), lane)
        gd[x] = 0.5 * ((ex + e0) + (ey + down(ey, 0))[0:16] + (ez + eb))
        gc[x] = (-1 / DT) * a_in[e, 0:16, :] * (m0 * r2[x] + s0 * r1[t])
        return ex

    ex = (sc[1, 0:16, :] - sc[2, 0:16, :]) * (later[1, 0:16, :] - later[0, 0:16, :])
    ex = ex + (sf[0, 0:16, :] - sf[1, 0:16, :]) * (p[0, 2, 0:16, :] - p[0, 1, 0:16, :])
    lax.fori_loop(0, n, fourth, ex, unroll=U4)


def coarse(x):
    x = jnp.transpose(x, (1, 0, 2))
    return jnp.pad(x, ((0, 0), (1, 1), (0, 0)))


def shards(c, d, s, cap, m, v, mask, cls, cw):
    n = c.shape[0]
    ends = [lax.axis_size(a) - 1 for a in ("gx", "gy", "gz")]
    idx = jnp.stack([lax.axis_index(a) for a in ("gx", "gy", "gz")]).astype(jnp.int32)
    fields = [pltpu.with_memory_space_constraint(f, pltpu.HBM) for f in (c, d, s, cap, m, v)]
    all_f, bx0, bx1, by0, by1, ys0, ys1 = call(
        pack_a,
        [(6, n, 16, 128)] + [(10, 16, 128)] * 2 + [(n + n // 4, 8, 128)] * 2 + [(6, 8, 128)] * 2,
        [SM] + [HB] * 6,
        (idx, *fields),
        [pltpu.SemaphoreType.DMA((6,))],
    )
    ys1 = swap(ys1, "gy", 1)
    ys0 = swap(ys0, "gy", 0)
    ry1 = swap(by1, "gy", 1)
    ry0 = swap(by0, "gy", 0)
    rx0 = swap(bx0, "gx", 0)
    rx1 = swap(bx1, "gx", 1)
    (tm,) = call(pack_t, [(6, 2, 16, 128)], [VM], (all_f,))
    t, e0, e1 = call(
        partial(pack_b, ends, n),
        [(6, 2, 24, 128), (4, 8, 128), (4, 8, 128)],
        [SM] + [VM] * 5,
        (idx, tm, rx0, rx1, ys0, ys1),
    )
    (p,) = call(
        partial(pack_c, ends),
        [(6, n + 4, 24, 128)],
        [SM] + [VM] * 5,
        (idx, all_f, rx0, rx1, ry0, ry1),
    )
    rz1 = swap(t, "gz", 1)
    rz0 = swap(t, "gz", 0)
    re0 = swap(e0, "gx", 0)
    re1 = swap(e1, "gx", 1)
    p, vox, h, a, later, later_z, r1, r2 = call(
        partial(forward, ends),
        [
            (6, n + 4, 24, 128),
            (2, 8, 128),
            (6, 2, 24, 128),
            (n + 4, 24, 128),
            (n + 2, 24, 128),
            (2, 24, 128),
            (n + 2, 16, 128),
            (n, 16, 128),
        ],
        [SM, SM] + [VM] * 8,
        (idx, cw, p, t, rz0, rz1, re0, re1, coarse(mask), coarse(cls)),
        [
            pltpu.VMEM((n + 2, 24, 128), F32),
            pltpu.VMEM((n + 2, 16, 128), F32),
            pltpu.VMEM((6, 2, 24, 128), F32),
            pltpu.VMEM((n // 8, 16, 128), F32),
        ],
        alias={2: 0},
    )
    ry1 = swap(vox, "gy", 1)
    ry0 = swap(vox, "gy", 0)
    rx0 = swap(vox, "gx", 0)
    rx1 = swap(vox, "gx", 1)
    vox, edge = call(
        partial(merge, ends), [(4, 8, 128), (2, 8, 128)], [SM] + [VM] * 5, (idx, vox, rx0, rx1, ry0, ry1), limit=1
    )
    rz1 = swap(vox, "gz", 1)
    rz0 = swap(vox, "gz", 0)
    re0 = swap(edge, "gx", 0)
    re1 = swap(edge, "gx", 1)
    gd, gc = call(
        partial(adjoint, ends),
        [(n, 16, 128)] * 2,
        [SM] + [VM] * 13,
        (idx, vox, rz0, rz1, re0, re1, p, t, h, a, later, later_z, r1, r2),
        [
            pltpu.VMEM((n // 8 + 2, 24, 128), F32),
            pltpu.VMEM((n + 4, 24, 128), F32),
            pltpu.VMEM((n + 2, 24, 128), F32),
            pltpu.VMEM((5, 2, 24, 128), F32),
        ],
    )
    return gd, gc


def solution(mesh):
    spec = P("gx", "gy", "gz")
    return jax.shard_map(
        shards, mesh=mesh, in_specs=(spec,) * 8 + (P(),), out_specs=(spec, spec), check_vma=False
    )
```

profile of v0, /device:TPU:32, one launch (start us, length us, event | category | flops | bytes accessed | tf_op | source)
XLA Modules:
  0.0 69.1 jit_solution(9311513318796464819)
XLA Ops:
  0.6 0.0 copy-start.1
  0.6 0.0 copy-start.2
  0.7 0.1 pad_add_fusion.idx
  0.7 3.0 %shard_map.104 = (f32[6,48,16,128]{3,2,1,0:T(8,128)S(1)}, f32[10,16,128]{2,1,0:T(8,128)S(1)}, f32[10,16,128]{2,1,0:T(8,128)S(1)}, f32[60,8,128]{2,1,0:T(8,128)S(...) custom-call(s32[3]{0:T(128)S(1)} %pad_add_fusion.idx, f32[48,16,128]{2,1,0:T(8,128)} %c.1, ...), custom_call_target="tpu_custom_call" | custom-call | tf_op jit(solution)/shard_map/pallas_call | solution.py:31
  3.7 0.1 collective-permute-start.2
  3.8 6.4 %collective-permute-start.3 = (f32[60,8,128]{2,1,0:T(8,128)S(1)}, f32[60,8,128]{2,1,0:T(8,128)S(1)}, u32[]{:S(2)}, u32[]{:S(2)}) collective-permute-start(f32[60,8,128]{2,1,0:T(8,128)S(1)} %get-tuple-element.26), channel_id=1, source_target_pairs={{16,32},{32,16},{48,0},{0,48},{17,33},{33,17},{49,1},{1,49},{18,34... | collective-permute-start | bytes 737288 | tf_op jit(solution)/shard_map/ppermute | solution.py:27
  10.2 1.6 %collective-permute-start = (f32[10,16,128]{2,1,0:T(8,128)S(1)}, f32[10,16,128]{2,1,0:T(8,128)S(1)}, u32[]{:S(2)}, u32[]{:S(2)}) collective-permute-start(f32[10,16,128]{2,1,0:T(8,128)S(1)} %get-tuple-element.23), channel_id=1, source_target_pairs={{0,64},{64,0},{128,192},{192,128},{1,65},{65,1},{129,193},{193,129... | collective-permute-start | bytes 245768 | tf_op jit(solution)/shard_map/ppermute | solution.py:27
  11.8 2.2 %collective-permute-start.1 = (f32[10,16,128]{2,1,0:T(8,128)S(1)}, f32[10,16,128]{2,1,0:T(8,128)S(1)}, u32[]{:S(2)}, u32[]{:S(2)}) collective-permute-start(f32[10,16,128]{2,1,0:T(8,128)S(1)} %get-tuple-element.24), channel_id=1, source_target_pairs={{64,128},{128,64},{192,0},{0,192},{65,129},{129,65},{193,1},{1,193... | collective-permute-start | bytes 245768 | tf_op jit(solution)/shard_map/ppermute | solution.py:27
  14.0 0.0 collective-permute-start.4
  14.0 1.2 %collective-permute-done.4.ys0 = f32[6,8,128]{2,1,0:T(8,128)S(1)} collective-permute-done((f32[6,8,128]{2,1,0:T(8,128)S(1)}, f32[6,8,128]{2,1,0:T(8,128)S(1)}, u32[]{:S(2)}, u32[]{:S(2)}) %collective-permute-start.4) | collective-permute-done | bytes 24608 | tf_op jit(solution)/shard_map/ppermute | solution.py:27
  15.2 0.0 collective-permute-start.5
  15.2 1.6 %shard_map.106.tm = f32[6,2,16,128]{3,2,1,0:T(8,128)S(1)} custom-call(f32[6,48,16,128]{3,2,1,0:T(8,128)S(1)} %get-tuple-element.22.all_f), custom_call_target="tpu_custom_call" | custom-call | tf_op jit(solution)/shard_map/pallas_call | solution.py:31
  16.8 0.0 copy-start
  16.8 5.6 %collective-permute-done.5.ys1 = f32[6,8,128]{2,1,0:T(8,128)S(1)} collective-permute-done((f32[6,8,128]{2,1,0:T(8,128)S(1)}, f32[6,8,128]{2,1,0:T(8,128)S(1)}, u32[]{:S(2)}, u32[]{:S(2)}) %collective-permute-start.5) | collective-permute-done | bytes 24608 | tf_op jit(solution)/shard_map/ppermute | solution.py:27
  22.4 0.0 collective-permute-done.rx0
  22.4 0.0 collective-permute-done.1.rx1
  22.4 0.6 shard_map.107
  23.1 1.5 %collective-permute-start.7 = (f32[6,2,24,128]{3,2,1,0:T(8,128)S(1)}, f32[6,2,24,128]{3,2,1,0:T(8,128)S(1)}, u32[]{:S(2)}, u32[]{:S(2)}) collective-permute-start(f32[6,2,24,128]{3,2,1,0:T(8,128)S(1)} %get-tuple-element.29.t), channel_id=1, source_target_pairs={{1,2},{2,1},{3,4},{4,3},{5,6},{6,5},{7,8},{8,7},{9,10},{10,9},{11,... | collective-permute-start | bytes 442376 | tf_op jit(solution)/shard_map/ppermute | solution.py:27
  24.5 4.6 %collective-permute-start.6 = (f32[6,2,24,128]{3,2,1,0:T(8,128)S(1)}, f32[6,2,24,128]{3,2,1,0:T(8,128)S(1)}, u32[]{:S(2)}, u32[]{:S(2)}) collective-permute-start(f32[6,2,24,128]{3,2,1,0:T(8,128)S(1)} %get-tuple-element.29.t), channel_id=1, source_target_pairs={{0,1},{1,0},{2,3},{3,2},{4,5},{5,4},{6,7},{7,6},{8,9},{9,8},{10,11... | collective-permute-start | bytes 442376 | tf_op jit(solution)/shard_map/ppermute | solution.py:27
  29.2 1.6 %collective-permute-start.8 = (f32[4,8,128]{2,1,0:T(8,128)S(1)}, f32[4,8,128]{2,1,0:T(8,128)S(1)}, u32[]{:S(2)}, u32[]{:S(2)}) collective-permute-start(f32[4,8,128]{2,1,0:T(8,128)S(1)} %get-tuple-element.30), channel_id=1, source_target_pairs={{0,64},{64,0},{128,192},{192,128},{1,65},{65,1},{129,193},{193,129... | collective-permute-start | bytes 49160 | tf_op jit(solution)/shard_map/ppermute | solution.py:27
  30.8 0.0 collective-permute-done.2.ry0
  30.8 0.0 collective-permute-start.9
  30.8 0.0 copy-done.1
  30.8 0.0 collective-permute-done.3.ry1
  30.8 0.9 %shard_map.105.p_in = f32[6,52,24,128]{3,2,1,0:T(8,128)S(1)} custom-call(s32[3]{0:T(128)S(1)} %pad_add_fusion.idx, f32[6,48,16,128]{3,2,1,0:T(8,128)S(1)} %get-tuple-element.22.all_f, f32[10,16,128]{2,1,0:T(8,128)S(1)} %collective-permute-done.rx0, f32[10,16,128]{2,1,0:T(8,128)S(1)} %collective-permute-done.1.rx1, ...), custom_call_target="tpu_custom_call" | custom-call | tf_op jit(solution)/shard_map/pallas_call | solution.py:31
  31.7 1.2 %collective-permute-done.8.re0 = f32[4,8,128]{2,1,0:T(8,128)S(1)} collective-permute-done((f32[4,8,128]{2,1,0:T(8,128)S(1)}, f32[4,8,128]{2,1,0:T(8,128)S(1)}, u32[]{:S(2)}, u32[]{:S(2)}) %collective-permute-start.8) | collective-permute-done | bytes 16416 | tf_op jit(solution)/shard_map/ppermute | solution.py:27
  32.9 2.8 %collective-permute-done.9.re1 = f32[4,8,128]{2,1,0:T(8,128)S(1)} collective-permute-done((f32[4,8,128]{2,1,0:T(8,128)S(1)}, f32[4,8,128]{2,1,0:T(8,128)S(1)}, u32[]{:S(2)}, u32[]{:S(2)}) %collective-permute-start.9) | collective-permute-done | bytes 16416 | tf_op jit(solution)/shard_map/ppermute | solution.py:27
  35.7 0.0 collective-permute-done.7.rz1
  35.7 0.5 collective-permute-done.6.rz0
  36.2 7.3 %shard_map.108 = (f32[6,52,24,128]{3,2,1,0:T(8,128)S(1)}, f32[2,8,128]{2,1,0:T(8,128)S(1)}, f32[6,2,24,128]{3,2,1,0:T(8,128)S(1)}, f32[52,24,128]{2,1,0:T(8,128)...) custom-call(s32[3]{0:T(128)S(1)} %pad_add_fusion.idx, ...), custom_call_target="tpu_custom_call", output_to_operand_aliasing={{0}: (2, {})} | custom-call | tf_op jit(solution)/shard_map/pallas_call | solution.py:31
  43.5 3.1 %collective-permute-start.13 = (f32[2,8,128]{2,1,0:T(8,128)S(1)}, f32[2,8,128]{2,1,0:T(8,128)S(1)}, u32[]{:S(2)}, u32[]{:S(2)}) collective-permute-start(f32[2,8,128]{2,1,0:T(8,128)S(1)} %get-tuple-element.32.own), channel_id=1, source_target_pairs={{16,32},{32,16},{48,0},{0,48},{17,33},{33,17},{49,1},{1,49},{18,34... | collective-permute-start | bytes 24584 | tf_op jit(solution)/shard_map/ppermute | solution.py:27
  46.6 1.3 %collective-permute-start.12 = (f32[2,8,128]{2,1,0:T(8,128)S(1)}, f32[2,8,128]{2,1,0:T(8,128)S(1)}, u32[]{:S(2)}, u32[]{:S(2)}) collective-permute-start(f32[2,8,128]{2,1,0:T(8,128)S(1)} %get-tuple-element.32.own), channel_id=1, source_target_pairs={{0,16},{16,0},{32,48},{48,32},{1,17},{17,1},{33,49},{49,33},{2,18}... | collective-permute-start | bytes 24584 | tf_op jit(solution)/shard_map/ppermute | solution.py:27
  47.9 2.1 %collective-permute-start.11 = (f32[2,8,128]{2,1,0:T(8,128)S(1)}, f32[2,8,128]{2,1,0:T(8,128)S(1)}, u32[]{:S(2)}, u32[]{:S(2)}) collective-permute-start(f32[2,8,128]{2,1,0:T(8,128)S(1)} %get-tuple-element.32.own), channel_id=1, source_target_pairs={{64,128},{128,64},{192,0},{0,192},{65,129},{129,65},{193,1},{1,193... | collective-permute-start | bytes 24584 | tf_op jit(solution)/shard_map/ppermute | solution.py:27
  50.0 0.0 collective-permute-start.10
  50.0 0.6 collective-permute-done.13.ry1
  50.6 0.0 collective-permute-done.12.ry0
  50.6 2.2 %collective-permute-done.11.rx1 = f32[2,8,128]{2,1,0:T(8,128)S(1)} collective-permute-done((f32[2,8,128]{2,1,0:T(8,128)S(1)}, f32[2,8,128]{2,1,0:T(8,128)S(1)}, u32[]{:S(2)}, u32[]{:S(2)}) %collective-permute-start.11) | collective-permute-done | bytes 8224 | tf_op jit(solution)/shard_map/ppermute | solution.py:27
  52.8 0.9 %collective-permute-done.10.rx0 = f32[2,8,128]{2,1,0:T(8,128)S(1)} collective-permute-done((f32[2,8,128]{2,1,0:T(8,128)S(1)}, f32[2,8,128]{2,1,0:T(8,128)S(1)}, u32[]{:S(2)}, u32[]{:S(2)}) %collective-permute-start.10) | collective-permute-done | bytes 8224 | tf_op jit(solution)/shard_map/ppermute | solution.py:27
  53.7 0.6 shard_map.109
  54.3 0.1 collective-permute-start.15
  54.4 4.1 %collective-permute-start.14 = (f32[4,8,128]{2,1,0:T(8,128)S(1)}, f32[4,8,128]{2,1,0:T(8,128)S(1)}, u32[]{:S(2)}, u32[]{:S(2)}) collective-permute-start(f32[4,8,128]{2,1,0:T(8,128)S(1)} %get-tuple-element.33.vox), channel_id=1, source_target_pairs={{0,1},{1,0},{2,3},{3,2},{4,5},{5,4},{6,7},{7,6},{8,9},{9,8},{10,11... | collective-permute-start | bytes 49160 | tf_op jit(solution)/shard_map/ppermute | solution.py:27
  58.4 1.2 %collective-permute-start.17 = (f32[2,8,128]{2,1,0:T(8,128)S(1)}, f32[2,8,128]{2,1,0:T(8,128)S(1)}, u32[]{:S(2)}, u32[]{:S(2)}) collective-permute-start(f32[2,8,128]{2,1,0:T(8,128)S(1)} %get-tuple-element.34), channel_id=1, source_target_pairs={{64,128},{128,64},{192,0},{0,192},{65,129},{129,65},{193,1},{1,193... | collective-permute-start | bytes 24584 | tf_op jit(solution)/shard_map/ppermute | solution.py:27
  59.7 0.0 collective-permute-start.16
  59.7 3.6 %collective-permute-done.17.re1 = f32[2,8,128]{2,1,0:T(8,128)S(1)} collective-permute-done((f32[2,8,128]{2,1,0:T(8,128)S(1)}, f32[2,8,128]{2,1,0:T(8,128)S(1)}, u32[]{:S(2)}, u32[]{:S(2)}) %collective-permute-start.17) | collective-permute-done | bytes 8224 | tf_op jit(solution)/shard_map/ppermute | solution.py:27
  63.3 0.0 collective-permute-done.16.re0
  63.3 0.0 collective-permute-done.15.rz1
  63.3 0.0 collective-permute-done.14.rz0
  63.3 5.8 %shard_map.110 = (f32[48,16,128]{2,1,0:T(8,128)}, f32[48,16,128]{2,1,0:T(8,128)}) custom-call(s32[3]{0:T(128)S(1)} %pad_add_fusion.idx, f32[4,8,128]{2,1,0:T(8,128)S(1)} %get-tuple-element.33.vox, f32[4,8,128]{2,1,0:T(8,128)S(1)} %collective-permute-done.14.rz0, f32[4,8,128]{2,1,0:T(8,128)S(1)} %collective-permute-done.15.rz1, ...), custom_call_target="tpu_custom_call" | custom-call | tf_op jit(solution)/shard_map/pallas_call | solution.py:31
  (6 shorter events, 0.0 us)
Async XLA Ops:
  0.6 30.1 %copy-start.1 = (s32[6,2,16]{2,1,0:T(2,128)S(1)}, s32[6,2,16]{2,1,0:T(2,128)}, u32[]{:S(2)}) copy-start(s32[6,2,16]{2,1,0:T(2,128)} %param.15) | copy-start | bytes 2308
  0.6 30.1 %copy-start.2 = (s32[6,2,16]{2,1,0:T(2,128)S(1)}, s32[6,2,16]{2,1,0:T(2,128)}, u32[]{:S(2)}) copy-start(s32[6,2,16]{2,1,0:T(2,128)} %param.16) | copy-start | bytes 2308
  3.7 27.0 %collective-permute-start.2 = (f32[60,8,128]{2,1,0:T(8,128)S(1)}, f32[60,8,128]{2,1,0:T(8,128)S(1)}, u32[]{:S(2)}, u32[]{:S(2)}) collective-permute-start(f32[60,8,128]{2,1,0:T(8,128)S(1)} %get-tuple-element.25), channel_id=1, source_target_pairs={{0,16},{16,0},{32,48},{48,32},{1,17},{17,1},{33,49},{49,33},{2,18}... | collective-permute-start | bytes 737288 | tf_op jit(solution)/shard_map/ppermute | solution.py:27
  3.8 27.0 %collective-permute-start.3 = (f32[60,8,128]{2,1,0:T(8,128)S(1)}, f32[60,8,128]{2,1,0:T(8,128)S(1)}, u32[]{:S(2)}, u32[]{:S(2)}) collective-permute-start(f32[60,8,128]{2,1,0:T(8,128)S(1)} %get-tuple-element.26), channel_id=1, source_target_pairs={{16,32},{32,16},{48,0},{0,48},{17,33},{33,17},{49,1},{1,49},{18,34... | collective-permute-start | bytes 737288 | tf_op jit(solution)/shard_map/ppermute | solution.py:27
  10.2 12.2 %collective-permute-start = (f32[10,16,128]{2,1,0:T(8,128)S(1)}, f32[10,16,128]{2,1,0:T(8,128)S(1)}, u32[]{:S(2)}, u32[]{:S(2)}) collective-permute-start(f32[10,16,128]{2,1,0:T(8,128)S(1)} %get-tuple-element.23), channel_id=1, source_target_pairs={{0,64},{64,0},{128,192},{192,128},{1,65},{65,1},{129,193},{193,129... | collective-permute-start | bytes 245768 | tf_op jit(solution)/shard_map/ppermute | solution.py:27
  11.8 10.6 %collective-permute-start.1 = (f32[10,16,128]{2,1,0:T(8,128)S(1)}, f32[10,16,128]{2,1,0:T(8,128)S(1)}, u32[]{:S(2)}, u32[]{:S(2)}) collective-permute-start(f32[10,16,128]{2,1,0:T(8,128)S(1)} %get-tuple-element.24), channel_id=1, source_target_pairs={{64,128},{128,64},{192,0},{0,192},{65,129},{129,65},{193,1},{1,193... | collective-permute-start | bytes 245768 | tf_op jit(solution)/shard_map/ppermute | solution.py:27
  14.0 1.2 %collective-permute-start.4 = (f32[6,8,128]{2,1,0:T(8,128)S(1)}, f32[6,8,128]{2,1,0:T(8,128)S(1)}, u32[]{:S(2)}, u32[]{:S(2)}) collective-permute-start(f32[6,8,128]{2,1,0:T(8,128)S(1)} %get-tuple-element.27), channel_id=1, source_target_pairs={{0,16},{16,0},{32,48},{48,32},{1,17},{17,1},{33,49},{49,33},{2,18}... | collective-permute-start | bytes 73736 | tf_op jit(solution)/shard_map/ppermute | solution.py:27
  15.2 7.2 %collective-permute-start.5 = (f32[6,8,128]{2,1,0:T(8,128)S(1)}, f32[6,8,128]{2,1,0:T(8,128)S(1)}, u32[]{:S(2)}, u32[]{:S(2)}) collective-permute-start(f32[6,8,128]{2,1,0:T(8,128)S(1)} %get-tuple-element.28), channel_id=1, source_target_pairs={{16,32},{32,16},{48,0},{0,48},{17,33},{33,17},{49,1},{1,49},{18,34... | collective-permute-start | bytes 73736 | tf_op jit(solution)/shard_map/ppermute | solution.py:27
  16.8 19.4 %copy-start = (f32[4]{0:T(128)S(1)}, f32[4]{0:T(128)}, u32[]{:S(2)}) copy-start(f32[4]{0:T(128)} %cw.1) | copy-start | bytes 52
  23.1 12.6 %collective-permute-start.7 = (f32[6,2,24,128]{3,2,1,0:T(8,128)S(1)}, f32[6,2,24,128]{3,2,1,0:T(8,128)S(1)}, u32[]{:S(2)}, u32[]{:S(2)}) collective-permute-start(f32[6,2,24,128]{3,2,1,0:T(8,128)S(1)} %get-tuple-element.29.t), channel_id=1, source_target_pairs={{1,2},{2,1},{3,4},{4,3},{5,6},{6,5},{7,8},{8,7},{9,10},{10,9},{11,... | collective-permute-start | bytes 442376 | tf_op jit(solution)/shard_map/ppermute | solution.py:27
  24.5 11.6 %collective-permute-start.6 = (f32[6,2,24,128]{3,2,1,0:T(8,128)S(1)}, f32[6,2,24,128]{3,2,1,0:T(8,128)S(1)}, u32[]{:S(2)}, u32[]{:S(2)}) collective-permute-start(f32[6,2,24,128]{3,2,1,0:T(8,128)S(1)} %get-tuple-element.29.t), channel_id=1, source_target_pairs={{0,1},{1,0},{2,3},{3,2},{4,5},{5,4},{6,7},{7,6},{8,9},{9,8},{10,11... | collective-permute-start | bytes 442376 | tf_op jit(solution)/shard_map/ppermute | solution.py:27
  29.2 3.7 %collective-permute-start.8 = (f32[4,8,128]{2,1,0:T(8,128)S(1)}, f32[4,8,128]{2,1,0:T(8,128)S(1)}, u32[]{:S(2)}, u32[]{:S(2)}) collective-permute-start(f32[4,8,128]{2,1,0:T(8,128)S(1)} %get-tuple-element.30), channel_id=1, source_target_pairs={{0,64},{64,0},{128,192},{192,128},{1,65},{65,1},{129,193},{193,129... | collective-permute-start | bytes 49160 | tf_op jit(solution)/shard_map/ppermute | solution.py:27
  30.8 5.0 %collective-permute-start.9 = (f32[4,8,128]{2,1,0:T(8,128)S(1)}, f32[4,8,128]{2,1,0:T(8,128)S(1)}, u32[]{:S(2)}, u32[]{:S(2)}) collective-permute-start(f32[4,8,128]{2,1,0:T(8,128)S(1)} %get-tuple-element.31), channel_id=1, source_target_pairs={{64,128},{128,64},{192,0},{0,192},{65,129},{129,65},{193,1},{1,193... | collective-permute-start | bytes 49160 | tf_op jit(solution)/shard_map/ppermute | solution.py:27
  43.5 7.1 %collective-permute-start.13 = (f32[2,8,128]{2,1,0:T(8,128)S(1)}, f32[2,8,128]{2,1,0:T(8,128)S(1)}, u32[]{:S(2)}, u32[]{:S(2)}) collective-permute-start(f32[2,8,128]{2,1,0:T(8,128)S(1)} %get-tuple-element.32.own), channel_id=1, source_target_pairs={{16,32},{32,16},{48,0},{0,48},{17,33},{33,17},{49,1},{1,49},{18,34... | collective-permute-start | bytes 24584 | tf_op jit(solution)/shard_map/ppermute | solution.py:27
  46.6 4.0 %collective-permute-start.12 = (f32[2,8,128]{2,1,0:T(8,128)S(1)}, f32[2,8,128]{2,1,0:T(8,128)S(1)}, u32[]{:S(2)}, u32[]{:S(2)}) collective-permute-start(f32[2,8,128]{2,1,0:T(8,128)S(1)} %get-tuple-element.32.own), channel_id=1, source_target_pairs={{0,16},{16,0},{32,48},{48,32},{1,17},{17,1},{33,49},{49,33},{2,18}... | collective-permute-start | bytes 24584 | tf_op jit(solution)/shard_map/ppermute | solution.py:27
  47.9 4.9 %collective-permute-start.11 = (f32[2,8,128]{2,1,0:T(8,128)S(1)}, f32[2,8,128]{2,1,0:T(8,128)S(1)}, u32[]{:S(2)}, u32[]{:S(2)}) collective-permute-start(f32[2,8,128]{2,1,0:T(8,128)S(1)} %get-tuple-element.32.own), channel_id=1, source_target_pairs={{64,128},{128,64},{192,0},{0,192},{65,129},{129,65},{193,1},{1,193... | collective-permute-start | bytes 24584 | tf_op jit(solution)/shard_map/ppermute | solution.py:27
  50.0 3.7 %collective-permute-start.10 = (f32[2,8,128]{2,1,0:T(8,128)S(1)}, f32[2,8,128]{2,1,0:T(8,128)S(1)}, u32[]{:S(2)}, u32[]{:S(2)}) collective-permute-start(f32[2,8,128]{2,1,0:T(8,128)S(1)} %get-tuple-element.32.own), channel_id=1, source_target_pairs={{0,64},{64,0},{128,192},{192,128},{1,65},{65,1},{129,193},{193,129... | collective-permute-start | bytes 24584 | tf_op jit(solution)/shard_map/ppermute | solution.py:27
  54.3 9.1 %collective-permute-start.15 = (f32[4,8,128]{2,1,0:T(8,128)S(1)}, f32[4,8,128]{2,1,0:T(8,128)S(1)}, u32[]{:S(2)}, u32[]{:S(2)}) collective-permute-start(f32[4,8,128]{2,1,0:T(8,128)S(1)} %get-tuple-element.33.vox), channel_id=1, source_target_pairs={{1,2},{2,1},{3,4},{4,3},{5,6},{6,5},{7,8},{8,7},{9,10},{10,9},{11,... | collective-permute-start | bytes 49160 | tf_op jit(solution)/shard_map/ppermute | solution.py:27
  54.4 9.0 %collective-permute-start.14 = (f32[4,8,128]{2,1,0:T(8,128)S(1)}, f32[4,8,128]{2,1,0:T(8,128)S(1)}, u32[]{:S(2)}, u32[]{:S(2)}) collective-permute-start(f32[4,8,128]{2,1,0:T(8,128)S(1)} %get-tuple-element.33.vox), channel_id=1, source_target_pairs={{0,1},{1,0},{2,3},{3,2},{4,5},{5,4},{6,7},{7,6},{8,9},{9,8},{10,11... | collective-permute-start | bytes 49160 | tf_op jit(solution)/shard_map/ppermute | solution.py:27
  58.4 4.9 %collective-permute-start.17 = (f32[2,8,128]{2,1,0:T(8,128)S(1)}, f32[2,8,128]{2,1,0:T(8,128)S(1)}, u32[]{:S(2)}, u32[]{:S(2)}) collective-permute-start(f32[2,8,128]{2,1,0:T(8,128)S(1)} %get-tuple-element.34), channel_id=1, source_target_pairs={{64,128},{128,64},{192,0},{0,192},{65,129},{129,65},{193,1},{1,193... | collective-permute-start | bytes 24584 | tf_op jit(solution)/shard_map/ppermute | solution.py:27
  59.7 3.7 %collective-permute-start.16 = (f32[2,8,128]{2,1,0:T(8,128)S(1)}, f32[2,8,128]{2,1,0:T(8,128)S(1)}, u32[]{:S(2)}, u32[]{:S(2)}) collective-permute-start(f32[2,8,128]{2,1,0:T(8,128)S(1)} %get-tuple-element.34), channel_id=1, source_target_pairs={{0,64},{64,0},{128,192},{192,128},{1,65},{65,1},{129,193},{193,129... | collective-permute-start | bytes 24584 | tf_op jit(solution)/shard_map/ppermute | solution.py:27
where the time goes:
time: 69.2 us; the launch traced here: 69.1 us
  starting transfers between devices  29.8 us (43%)
  Pallas kernels  19.8 us (29%)
  waiting for transfers between devices  18.6 us (27%)
  between operations  0.78 us (1%)
    ppermute x18, starting transfers between devices, swap(): return lax.ppermute(value, axis, swap_pairs(lax.axis_size(axis), first))  29.8 us
    pallas_call x7, Pallas kernels, call(): pl.pallas_call(body, out_shape=[jax.ShapeDtypeStruct(s, F32) for s in out...  19.8 us
    ppermute x18, waiting for transfers between devices, swap(): return lax.ppermute(value, axis, swap_pairs(lax.axis_size(axis), first))  18.6 us
  transfers between devices with their start and end apart: 18, of which 9 were waited for; matrix products, arithmetic and copies ran while one was open for 0% of the time, Pallas kernels for 5%

commit v1 on v0

--- a/solution.py
+++ b/solution.py
@@ -9,6 +9,7 @@
 
 
 DT = 0.1
+CHUNKS = 1
 U1, U2, U3, U4 = (5, 4, 10, 8)
 F32 = jnp.float32
 VM = pl.BlockSpec(memory_space=pltpu.VMEM)
@@ -16,15 +17,19 @@
 HB = pl.BlockSpec(memory_space=pltpu.HBM)
 
 
-def swap_pairs(size, first):
+def swap_pairs(size, first, ends=True):
     pairs = []
-    for i in range(first, size, 2):
+    for i in range(first, size if ends else size - 1, 2):
         pairs += [(i, (i + 1) % size), ((i + 1) % size, i)]
     return pairs
 
 
-def swap(value, axis, first):
-    return lax.ppermute(value, axis, swap_pairs(lax.axis_size(axis), first))
+def swap(value, axis, first, name):
+    ends = name not in PARTIAL
+    return lax.ppermute(value, axis, swap_pairs(lax.axis_size(axis), first, ends))
+
+
+PARTIAL = ()
 
 
 def call(body, outs, specs, args, scratch=(), limit=24, alias=None):
@@ -76,8 +81,12 @@
     xeven = is_even(idx, 0)
     yeven = is_even(idx, 1)
     row = rows((8, 128))
+    part = n // CHUNKS
     copies = [
-        pltpu.make_async_copy(ref, all_f.at[f], sems.at[f])
+        pltpu.make_async_copy(
+            ref.at[pl.ds(k * part, part)], all_f.at[f, pl.ds(k * part, part)], sems.at[f * CHUNKS + k]
+        )
+        for k in range(CHUNKS)
         for f, ref in enumerate((c, d, s, cap, m, v))
     ]
     for copy in copies:
@@ -176,8 +185,10 @@
     return jnp.where(row < 4, rolled(hi, -2 * f, 0), rolled(lo, 6 - 2 * f, 0))
 
 
-def pack_b(ends, planes, idx, tm, rx0, rx1, ys0, ys1, t, e0, e1):
+def pack_b(ends, planes, idx, tm, rx0, rx1, ys0, ys1, t, b0, b1, e0, e1):
     xeven = is_even(idx, 0)
+    zeven = is_even(idx, 2)
+    left = lanes((24, 128)) % 4 < 2
     row = rows((8, 128))
     lane = lanes((16, 128))
     tiles = [picked(ends, idx, 1, ys0[k], ys1[k]) for k in range(6)]
@@ -193,13 +204,18 @@
                 t[f, col, 16:24, :] = jnp.zeros((8, 128), F32)
             else:
                 t[f, col, 16:24, :] = jnp.where(row < 4, tiles[2 + col][1], tiles[2 + col][0])
+        one, two = (t[f, 0], t[f, 1])
+        hi = jnp.where(left, one, pltpu.roll(two, 2, 1))
+        lo = jnp.where(left, pltpu.roll(one, 126, 1), two)
+        b0[f] = jnp.where(zeven, hi, lo)
+        b1[f] = jnp.where(zeven, lo, hi)
     for f in range(4):
         lo, hi = (third(tiles[k][1], tiles[k][0], f) for k in (4, 5))
         e0[f] = jnp.where(xeven, hi, lo)
         e1[f] = jnp.where(xeven, lo, hi)
 
 
-def pack_c(ends, idx, all_f, rx0, rx1, ry0, ry1, p):
+def pack_c(ends, idx, all_f, rx0, rx1, ry0, ry1, p, a_out):
     n = all_f.shape[1]
     row = rows((8, 128))
     zero = jnp.zeros((8, 128), F32)
@@ -234,6 +250,12 @@
         for e in (0, 1, n + 2, n + 3):
             p[f, e, 16:24, :] = zero
 
+    def make(e, _):
+        a_out[e] = inverse(p[3, e])
+        return 0
+
+    lax.fori_loop(0, n + 4, make, 0, unroll=4)
+
 
 def wide(ref):
     return jnp.concatenate([ref[0], ref[1]], axis=1)
@@ -275,19 +297,21 @@
 
 
 def forward(
-    ends, idx, cw, p_in, t, rz0, rz1, re0, re1, mask, cls,
+    ends, idx, cw, p_in, a_in, t, rz0, rz1, re0, re1, mask, cls,
     p, v_out, h, a_out, later, later_z, r1, r2, tang, q_s, m, cs,
 ):
     n = r2.shape[0]
     for f in range(4):
         p[f, 1, 16:24, :], p[f, n + 2, 16:24, :] = picked(ends, idx, 0, re0[f], re1[f])
+    for e in (1, n + 2):
+        a_out[e, 16:24, :] = inverse(p[3, e, 16:24, :])
 
     slot = lanes((24, 256)) % 4
     own, halo = ([], [])
     for f in range(6):
-        for col in range(2):
-            lo, hi = picked(ends, idx, 2, rz0[f, col], rz1[f, col])
-            h[f, col] = jnp.where(slot[:, 0:128] < 2, lo, hi)
+        lo, hi = picked(ends, idx, 2, rz0[f], rz1[f])
+        h[f, 0] = jnp.where(slot[:, 0:128] < 2, lo, pltpu.roll(hi, 2, 1))
+        h[f, 1] = jnp.where(slot[:, 0:128] < 2, pltpu.roll(lo, 126, 1), hi)
         own.append(wide(t.at[f]))
         halo.append(wide(h.at[f]))
     near = [
@@ -304,11 +328,6 @@
     for at, value in enumerate((halo[0], halo[1], halo[2], halo[5], lz, tz)):
         to_ends(m, at, value, slot)
 
-    def make(e, _):
-        a_out[e] = inverse(p[3, e])
-        return 0
-
-    lax.fori_loop(0, n + 4, make, 0, unroll=4)
     lane = lanes((24, 128))
 
     def first(t, carry):
@@ -539,31 +558,31 @@
         [(6, n, 16, 128)] + [(10, 16, 128)] * 2 + [(n + n // 4, 8, 128)] * 2 + [(6, 8, 128)] * 2,
         [SM] + [HB] * 6,
         (idx, *fields),
-        [pltpu.SemaphoreType.DMA((6,))],
-    )
-    ys1 = swap(ys1, "gy", 1)
-    ys0 = swap(ys0, "gy", 0)
-    ry1 = swap(by1, "gy", 1)
-    ry0 = swap(by0, "gy", 0)
-    rx0 = swap(bx0, "gx", 0)
-    rx1 = swap(bx1, "gx", 1)
+        [pltpu.SemaphoreType.DMA((6 * CHUNKS,))],
+    )
+    ys1 = swap(ys1, "gy", 1, "small_y1")
+    ys0 = swap(ys0, "gy", 0, "small_y0")
+    ry1 = swap(by1, "gy", 1, "large_y1")
+    ry0 = swap(by0, "gy", 0, "large_y0")
+    rx0 = swap(bx0, "gx", 0, "face_x0")
+    rx1 = swap(bx1, "gx", 1, "face_x1")
     (tm,) = call(pack_t, [(6, 2, 16, 128)], [VM], (all_f,))
-    t, e0, e1 = call(
+    t, bz0, bz1, e0, e1 = call(
         partial(pack_b, ends, n),
-        [(6, 2, 24, 128), (4, 8, 128), (4, 8, 128)],
+        [(6, 2, 24, 128), (6, 24, 128), (6, 24, 128), (4, 8, 128), (4, 8, 128)],
         [SM] + [VM] * 5,
         (idx, tm, rx0, rx1, ys0, ys1),
     )
-    (p,) = call(
+    p, a = call(
         partial(pack_c, ends),
-        [(6, n + 4, 24, 128)],
+        [(6, n + 4, 24, 128), (n + 4, 24, 128)],
         [SM] + [VM] * 5,
         (idx, all_f, rx0, rx1, ry0, ry1),
     )
-    rz1 = swap(t, "gz", 1)
-    rz0 = swap(t, "gz", 0)
-    re0 = swap(e0, "gx", 0)
-    re1 = swap(e1, "gx", 1)
+    rz1 = swap(bz1, "gz", 1, "ends_z1")
+    rz0 = swap(bz0, "gz", 0, "ends_z0")
+    re0 = swap(e0, "gx", 0, "rows_x0")
+    re1 = swap(e1, "gx", 1, "rows_x1")
     p, vox, h, a, later, later_z, r1, r2 = call(
         partial(forward, ends),
         [
@@ -576,27 +595,27 @@
             (n + 2, 16, 128),
             (n, 16, 128),
         ],
-        [SM, SM] + [VM] * 8,
-        (idx, cw, p, t, rz0, rz1, re0, re1, coarse(mask), coarse(cls)),
+        [SM, SM] + [VM] * 9,
+        (idx, cw, p, a, t, rz0, rz1, re0, re1, coarse(mask), coarse(cls)),
         [
             pltpu.VMEM((n + 2, 24, 128), F32),
             pltpu.VMEM((n + 2, 16, 128), F32),
             pltpu.VMEM((6, 2, 24, 128), F32),
             pltpu.VMEM((n // 8, 16, 128), F32),
         ],
-        alias={2: 0},
-    )
-    ry1 = swap(vox, "gy", 1)
-    ry0 = swap(vox, "gy", 0)
-    rx0 = swap(vox, "gx", 0)
-    rx1 = swap(vox, "gx", 1)
+        alias={2: 0, 3: 3},
+    )
+    ry1 = swap(vox, "gy", 1, "voxel_y1")
+    ry0 = swap(vox, "gy", 0, "voxel_y0")
+    rx0 = swap(vox, "gx", 0, "voxel_x0")
+    rx1 = swap(vox, "gx", 1, "voxel_x1")
     vox, edge = call(
         partial(merge, ends), [(4, 8, 128), (2, 8, 128)], [SM] + [VM] * 5, (idx, vox, rx0, rx1, ry0, ry1), limit=1
     )
-    rz1 = swap(vox, "gz", 1)
-    rz0 = swap(vox, "gz", 0)
-    re0 = swap(edge, "gx", 0)
-    re1 = swap(edge, "gx", 1)
+    rz1 = swap(vox, "gz", 1, "voxel_z1")
+    rz0 = swap(vox, "gz", 0, "voxel_z0")
+    re0 = swap(edge, "gx", 0, "corner_x0")
+    re1 = swap(edge, "gx", 1, "corner_x1")
     gd, gc = call(
         partial(adjoint, ends),
         [(n, 16, 128)] * 2,

time: 69.2 us -> 68.7 us (level)
  waiting for transfers between devices: 18.6 us -> 17.2 us
  starting transfers between devices: 29.8 us -> 30.5 us
    ppermute x18, waiting for transfers between devices: 18.6 us -> 17.2 us  [swap(): lax.ppermute(value, axis, swap_pairs(lax.axis_size(axis), first, ends))]
  transfers between devices with their start and end apart: 18 -> 18, of which waited for: 9 -> 8; matrix products, arithmetic and copies ran while one was open for 0% -> 0% of each run, Pallas kernels for 5% -> 5%
where the time goes in v1:
time: 68.7 us; the launch traced here: 68.6 us
  starting transfers between devices  30.5 us (44%)
  Pallas kernels  20 us (29%)
  waiting for transfers between devices  17.2 us (25%)
  between operations  0.75 us (1%)
    ppermute x18, starting transfers between devices, swap(): lax.ppermute(value, axis, swap_pairs(lax.axis_size(axis), first, ends))  30.5 us
    pallas_call x7, Pallas kernels, call(): pl.pallas_call(body, out_shape=[jax.ShapeDtypeStruct(s, F32) for s in out...  20 us
    ppermute x18, waiting for transfers between devices, swap(): lax.ppermute(value, axis, swap_pairs(lax.axis_size(axis), first, ends))  17.2 us
  transfers between devices with their start and end apart: 18, of which 8 were waited for; matrix products, arithmetic and copies ran while one was open for 0% of the time, Pallas kernels for 5%

profile of v1, /device:TPU:32, one launch (start us, length us, event | category | flops | bytes accessed | tf_op | source)
XLA Modules:
  0.0 68.6 jit_solution(6518780712502535782)
XLA Ops:
  0.6 0.0 copy-start.1
  0.6 0.0 copy-start.2
  0.7 0.1 pad_add_fusion.idx
  0.7 3.0 %shard_map.104 = (f32[6,48,16,128]{3,2,1,0:T(8,128)S(1)}, f32[10,16,128]{2,1,0:T(8,128)S(1)}, f32[10,16,128]{2,1,0:T(8,128)S(1)}, f32[60,8,128]{2,1,0:T(8,128)S(...) custom-call(s32[3]{0:T(128)S(1)} %pad_add_fusion.idx, f32[48,16,128]{2,1,0:T(8,128)} %c.1, ...), custom_call_target="tpu_custom_call" | custom-call | tf_op jit(solution)/shard_map/pallas_call | solution.py:36
  3.7 0.1 collective-permute-start.2
  3.8 6.4 %collective-permute-start.3 = (f32[60,8,128]{2,1,0:T(8,128)S(1)}, f32[60,8,128]{2,1,0:T(8,128)S(1)}, u32[]{:S(2)}, u32[]{:S(2)}) collective-permute-start(f32[60,8,128]{2,1,0:T(8,128)S(1)} %get-tuple-element.30), channel_id=1, source_target_pairs={{16,32},{32,16},{48,0},{0,48},{17,33},{33,17},{49,1},{1,49},{18,34... | collective-permute-start | bytes 737288 | tf_op jit(solution)/shard_map/ppermute | solution.py:29
  10.2 1.6 %collective-permute-start = (f32[10,16,128]{2,1,0:T(8,128)S(1)}, f32[10,16,128]{2,1,0:T(8,128)S(1)}, u32[]{:S(2)}, u32[]{:S(2)}) collective-permute-start(f32[10,16,128]{2,1,0:T(8,128)S(1)} %get-tuple-element.27), channel_id=1, source_target_pairs={{0,64},{64,0},{128,192},{192,128},{1,65},{65,1},{129,193},{193,129... | collective-permute-start | bytes 245768 | tf_op jit(solution)/shard_map/ppermute | solution.py:29
  11.8 2.2 %collective-permute-start.1 = (f32[10,16,128]{2,1,0:T(8,128)S(1)}, f32[10,16,128]{2,1,0:T(8,128)S(1)}, u32[]{:S(2)}, u32[]{:S(2)}) collective-permute-start(f32[10,16,128]{2,1,0:T(8,128)S(1)} %get-tuple-element.28), channel_id=1, source_target_pairs={{64,128},{128,64},{192,0},{0,192},{65,129},{129,65},{193,1},{1,193... | collective-permute-start | bytes 245768 | tf_op jit(solution)/shard_map/ppermute | solution.py:29
  14.0 0.0 collective-permute-start.4
  14.0 1.2 %collective-permute-done.4.ys0 = f32[6,8,128]{2,1,0:T(8,128)S(1)} collective-permute-done((f32[6,8,128]{2,1,0:T(8,128)S(1)}, f32[6,8,128]{2,1,0:T(8,128)S(1)}, u32[]{:S(2)}, u32[]{:S(2)}) %collective-permute-start.4) | collective-permute-done | bytes 24608 | tf_op jit(solution)/shard_map/ppermute | solution.py:29
  15.2 0.0 collective-permute-start.5
  15.2 1.6 %shard_map.106.tm = f32[6,2,16,128]{3,2,1,0:T(8,128)S(1)} custom-call(f32[6,48,16,128]{3,2,1,0:T(8,128)S(1)} %get-tuple-element.26.all_f), custom_call_target="tpu_custom_call" | custom-call | tf_op jit(solution)/shard_map/pallas_call | solution.py:36
  16.8 5.6 %collective-permute-done.5.ys1 = f32[6,8,128]{2,1,0:T(8,128)S(1)} collective-permute-done((f32[6,8,128]{2,1,0:T(8,128)S(1)}, f32[6,8,128]{2,1,0:T(8,128)S(1)}, u32[]{:S(2)}, u32[]{:S(2)}) %collective-permute-start.5) | collective-permute-done | bytes 24608 | tf_op jit(solution)/shard_map/ppermute | solution.py:29
  22.4 0.0 collective-permute-done.rx0
  22.4 0.0 collective-permute-done.1.rx1
  22.4 0.7 %shard_map.107 = (f32[6,2,24,128]{3,2,1,0:T(8,128)S(1)}, f32[6,24,128]{2,1,0:T(8,128)S(1)}, f32[6,24,128]{2,1,0:T(8,128)S(1)}, f32[4,8,128]{2,1,0:T(8,128)S(1)}, f32[4,8,128]{2,1,0:T(8,128)S(1)}) custom-call(s32[3]{0:T(128)S(1)} %pad_add_fusion.idx, f32[6,2,16,128]{3,2,1,0:T(8,128)S(1)} %shard_map.106.tm, f32[10,16,128]{2,1,0:T(8,128)S(1)} %collective-permute-done.rx0, ...), custom_call_target="tpu_custom_call" | custom-call | tf_op jit(solution)/shard_map/pallas_call | solution.py:36
  23.1 1.0 %collective-permute-start.6 = (f32[6,24,128]{2,1,0:T(8,128)S(1)}, f32[6,24,128]{2,1,0:T(8,128)S(1)}, u32[]{:S(2)}, u32[]{:S(2)}) collective-permute-start(f32[6,24,128]{2,1,0:T(8,128)S(1)} %get-tuple-element.36), channel_id=1, source_target_pairs={{0,1},{1,0},{2,3},{3,2},{4,5},{5,4},{6,7},{7,6},{8,9},{9,8},{10,11... | collective-permute-start | bytes 221192 | tf_op jit(solution)/shard_map/ppermute | solution.py:29
  24.2 2.0 %collective-permute-start.7 = (f32[6,24,128]{2,1,0:T(8,128)S(1)}, f32[6,24,128]{2,1,0:T(8,128)S(1)}, u32[]{:S(2)}, u32[]{:S(2)}) collective-permute-start(f32[6,24,128]{2,1,0:T(8,128)S(1)} %get-tuple-element.37), channel_id=1, source_target_pairs={{1,2},{2,1},{3,4},{4,3},{5,6},{6,5},{7,8},{8,7},{9,10},{10,9},{11,... | collective-permute-start | bytes 221192 | tf_op jit(solution)/shard_map/ppermute | solution.py:29
  26.2 1.6 %collective-permute-start.8 = (f32[4,8,128]{2,1,0:T(8,128)S(1)}, f32[4,8,128]{2,1,0:T(8,128)S(1)}, u32[]{:S(2)}, u32[]{:S(2)}) collective-permute-start(f32[4,8,128]{2,1,0:T(8,128)S(1)} %get-tuple-element.38), channel_id=1, source_target_pairs={{0,64},{64,0},{128,192},{192,128},{1,65},{65,1},{129,193},{193,129... | collective-permute-start | bytes 49160 | tf_op jit(solution)/shard_map/ppermute | solution.py:29
  27.7 0.0 collective-permute-done.2.ry0
  27.7 0.7 %collective-permute-start.9 = (f32[4,8,128]{2,1,0:T(8,128)S(1)}, f32[4,8,128]{2,1,0:T(8,128)S(1)}, u32[]{:S(2)}, u32[]{:S(2)}) collective-permute-start(f32[4,8,128]{2,1,0:T(8,128)S(1)} %get-tuple-element.39), channel_id=1, source_target_pairs={{64,128},{128,64},{192,0},{0,192},{65,129},{129,65},{193,1},{1,193... | collective-permute-start | bytes 49160 | tf_op jit(solution)/shard_map/ppermute | solution.py:29
  28.5 0.0 copy-done.1
  28.5 0.0 copy-done.2
  28.5 0.0 collective-permute-done.3.ry1
  28.5 1.1 %shard_map.105 = (f32[6,52,24,128]{3,2,1,0:T(8,128)S(1)}, f32[52,24,128]{2,1,0:T(8,128)S(1)}) custom-call(s32[3]{0:T(128)S(1)} %pad_add_fusion.idx, f32[6,48,16,128]{3,2,1,0:T(8,128)S(1)} %get-tuple-element.26.all_f, f32[10,16,128]{2,1,0:T(8,128)S(1)} %collective-permute-done.rx0, f32[10,16,128]{2,1,0:T(8,128)S(1)} %collective-permute-done.1.rx1, ...), custom_call_target="tpu_custom_call" | custom-call | tf_op jit(solution)/shard_map/pallas_call | solution.py:36
  29.6 0.3 collective-permute-done.8.re0
  29.9 2.8 %collective-permute-done.9.re1 = f32[4,8,128]{2,1,0:T(8,128)S(1)} collective-permute-done((f32[4,8,128]{2,1,0:T(8,128)S(1)}, f32[4,8,128]{2,1,0:T(8,128)S(1)}, u32[]{:S(2)}, u32[]{:S(2)}) %collective-permute-start.9) | collective-permute-done | bytes 16416 | tf_op jit(solution)/shard_map/ppermute | solution.py:29
  32.7 0.0 collective-permute-done.6.rz0
  32.7 0.0 collective-permute-done.7.rz1
  32.7 7.2 %shard_map.108 = (f32[6,52,24,128]{3,2,1,0:T(8,128)S(1)}, f32[2,8,128]{2,1,0:T(8,128)S(1)}, f32[6,2,24,128]{3,2,1,0:T(8,128)S(1)}, f32[52,24,128]{2,1,0:T(8,128)...) custom-call(s32[3]{0:T(128)S(1)} %pad_add_fusion.idx, ...), custom_call_target="tpu_custom_call", output_to_operand_aliasing={{0}: (2, {}), {3}: (3, {})} | custom-call | tf_op jit(solution)/shard_map/pallas_call | solution.py:36
  39.9 2.0 %collective-permute-start.13 = (f32[2,8,128]{2,1,0:T(8,128)S(1)}, f32[2,8,128]{2,1,0:T(8,128)S(1)}, u32[]{:S(2)}, u32[]{:S(2)}) collective-permute-start(f32[2,8,128]{2,1,0:T(8,128)S(1)} %get-tuple-element.40.own), channel_id=1, source_target_pairs={{16,32},{32,16},{48,0},{0,48},{17,33},{33,17},{49,1},{1,49},{18,34... | collective-permute-start | bytes 24584 | tf_op jit(solution)/shard_map/ppermute | solution.py:29
  41.9 2.5 %collective-permute-start.12 = (f32[2,8,128]{2,1,0:T(8,128)S(1)}, f32[2,8,128]{2,1,0:T(8,128)S(1)}, u32[]{:S(2)}, u32[]{:S(2)}) collective-permute-start(f32[2,8,128]{2,1,0:T(8,128)S(1)} %get-tuple-element.40.own), channel_id=1, source_target_pairs={{0,16},{16,0},{32,48},{48,32},{1,17},{17,1},{33,49},{49,33},{2,18}... | collective-permute-start | bytes 24584 | tf_op jit(solution)/shard_map/ppermute | solution.py:29
  44.5 1.5 %collective-permute-start.11 = (f32[2,8,128]{2,1,0:T(8,128)S(1)}, f32[2,8,128]{2,1,0:T(8,128)S(1)}, u32[]{:S(2)}, u32[]{:S(2)}) collective-permute-start(f32[2,8,128]{2,1,0:T(8,128)S(1)} %get-tuple-element.40.own), channel_id=1, source_target_pairs={{64,128},{128,64},{192,0},{0,192},{65,129},{129,65},{193,1},{1,193... | collective-permute-start | bytes 24584 | tf_op jit(solution)/shard_map/ppermute | solution.py:29
  46.0 0.0 collective-permute-start.10
  46.0 1.0 %collective-permute-done.13.ry1 = f32[2,8,128]{2,1,0:T(8,128)S(1)} collective-permute-done((f32[2,8,128]{2,1,0:T(8,128)S(1)}, f32[2,8,128]{2,1,0:T(8,128)S(1)}, u32[]{:S(2)}, u32[]{:S(2)}) %collective-permute-start.13) | collective-permute-done | bytes 8224 | tf_op jit(solution)/shard_map/ppermute | solution.py:29
  47.0 0.0 collective-permute-done.12.ry0
  47.0 2.3 %collective-permute-done.11.rx1 = f32[2,8,128]{2,1,0:T(8,128)S(1)} collective-permute-done((f32[2,8,128]{2,1,0:T(8,128)S(1)}, f32[2,8,128]{2,1,0:T(8,128)S(1)}, u32[]{:S(2)}, u32[]{:S(2)}) %collective-permute-start.11) | collective-permute-done | bytes 8224 | tf_op jit(solution)/shard_map/ppermute | solution.py:29
  49.3 0.3 collective-permute-done.10.rx0
  49.6 0.6 shard_map.109
  50.2 1.3 %collective-permute-start.15 = (f32[4,8,128]{2,1,0:T(8,128)S(1)}, f32[4,8,128]{2,1,0:T(8,128)S(1)}, u32[]{:S(2)}, u32[]{:S(2)}) collective-permute-start(f32[4,8,128]{2,1,0:T(8,128)S(1)} %get-tuple-element.41.vox), channel_id=1, source_target_pairs={{1,2},{2,1},{3,4},{4,3},{5,6},{6,5},{7,8},{8,7},{9,10},{10,9},{11,... | collective-permute-start | bytes 49160 | tf_op jit(solution)/shard_map/ppermute | solution.py:29
  51.5 6.4 %collective-permute-start.14 = (f32[4,8,128]{2,1,0:T(8,128)S(1)}, f32[4,8,128]{2,1,0:T(8,128)S(1)}, u32[]{:S(2)}, u32[]{:S(2)}) collective-permute-start(f32[4,8,128]{2,1,0:T(8,128)S(1)} %get-tuple-element.41.vox), channel_id=1, source_target_pairs={{0,1},{1,0},{2,3},{3,2},{4,5},{5,4},{6,7},{7,6},{8,9},{9,8},{10,11... | collective-permute-start | bytes 49160 | tf_op jit(solution)/shard_map/ppermute | solution.py:29
  57.9 1.2 %collective-permute-start.17 = (f32[2,8,128]{2,1,0:T(8,128)S(1)}, f32[2,8,128]{2,1,0:T(8,128)S(1)}, u32[]{:S(2)}, u32[]{:S(2)}) collective-permute-start(f32[2,8,128]{2,1,0:T(8,128)S(1)} %get-tuple-element.42), channel_id=1, source_target_pairs={{64,128},{128,64},{192,0},{0,192},{65,129},{129,65},{193,1},{1,193... | collective-permute-start | bytes 24584 | tf_op jit(solution)/shard_map/ppermute | solution.py:29
  59.1 0.0 collective-permute-start.16
  59.1 3.6 %collective-permute-done.17.re1 = f32[2,8,128]{2,1,0:T(8,128)S(1)} collective-permute-done((f32[2,8,128]{2,1,0:T(8,128)S(1)}, f32[2,8,128]{2,1,0:T(8,128)S(1)}, u32[]{:S(2)}, u32[]{:S(2)}) %collective-permute-start.17) | collective-permute-done | bytes 8224 | tf_op jit(solution)/shard_map/ppermute | solution.py:29
  62.8 0.0 collective-permute-done.16.re0
  62.8 0.0 collective-permute-done.15.rz1
  62.8 0.0 collective-permute-done.14.rz0
  62.8 5.8 %shard_map.110 = (f32[48,16,128]{2,1,0:T(8,128)}, f32[48,16,128]{2,1,0:T(8,128)}) custom-call(s32[3]{0:T(128)S(1)} %pad_add_fusion.idx, f32[4,8,128]{2,1,0:T(8,128)S(1)} %get-tuple-element.41.vox, f32[4,8,128]{2,1,0:T(8,128)S(1)} %collective-permute-done.14.rz0, f32[4,8,128]{2,1,0:T(8,128)S(1)} %collective-permute-done.15.rz1, ...), custom_call_target="tpu_custom_call" | custom-call | tf_op jit(solution)/shard_map/pallas_call | solution.py:36
  (6 shorter events, 0.0 us)
Async XLA Ops:
  0.6 27.8 %copy-start.1 = (s32[6,2,16]{2,1,0:T(2,128)S(1)}, s32[6,2,16]{2,1,0:T(2,128)}, u32[]{:S(2)}) copy-start(s32[6,2,16]{2,1,0:T(2,128)} %param.15) | copy-start | bytes 2308
  0.6 27.8 %copy-start.2 = (s32[6,2,16]{2,1,0:T(2,128)S(1)}, s32[6,2,16]{2,1,0:T(2,128)}, u32[]{:S(2)}) copy-start(s32[6,2,16]{2,1,0:T(2,128)} %param.16) | copy-start | bytes 2308
  0.7 32.0 %copy-start = (f32[4]{0:T(128)S(1)}, f32[4]{0:T(128)}, u32[]{:S(2)}) copy-start(f32[4]{0:T(128)} %cw.1) | copy-start | bytes 52
  3.7 24.0 %collective-permute-start.2 = (f32[60,8,128]{2,1,0:T(8,128)S(1)}, f32[60,8,128]{2,1,0:T(8,128)S(1)}, u32[]{:S(2)}, u32[]{:S(2)}) collective-permute-start(f32[60,8,128]{2,1,0:T(8,128)S(1)} %get-tuple-element.29), channel_id=1, source_target_pairs={{0,16},{16,0},{32,48},{48,32},{1,17},{17,1},{33,49},{49,33},{2,18}... | collective-permute-start | bytes 737288 | tf_op jit(solution)/shard_map/ppermute | solution.py:29
  3.8 24.7 %collective-permute-start.3 = (f32[60,8,128]{2,1,0:T(8,128)S(1)}, f32[60,8,128]{2,1,0:T(8,128)S(1)}, u32[]{:S(2)}, u32[]{:S(2)}) collective-permute-start(f32[60,8,128]{2,1,0:T(8,128)S(1)} %get-tuple-element.30), channel_id=1, source_target_pairs={{16,32},{32,16},{48,0},{0,48},{17,33},{33,17},{49,1},{1,49},{18,34... | collective-permute-start | bytes 737288 | tf_op jit(solution)/shard_map/ppermute | solution.py:29
  10.2 12.2 %collective-permute-start = (f32[10,16,128]{2,1,0:T(8,128)S(1)}, f32[10,16,128]{2,1,0:T(8,128)S(1)}, u32[]{:S(2)}, u32[]{:S(2)}) collective-permute-start(f32[10,16,128]{2,1,0:T(8,128)S(1)} %get-tuple-element.27), channel_id=1, source_target_pairs={{0,64},{64,0},{128,192},{192,128},{1,65},{65,1},{129,193},{193,129... | collective-permute-start | bytes 245768 | tf_op jit(solution)/shard_map/ppermute | solution.py:29
  11.8 10.6 %collective-permute-start.1 = (f32[10,16,128]{2,1,0:T(8,128)S(1)}, f32[10,16,128]{2,1,0:T(8,128)S(1)}, u32[]{:S(2)}, u32[]{:S(2)}) collective-permute-start(f32[10,16,128]{2,1,0:T(8,128)S(1)} %get-tuple-element.28), channel_id=1, source_target_pairs={{64,128},{128,64},{192,0},{0,192},{65,129},{129,65},{193,1},{1,193... | collective-permute-start | bytes 245768 | tf_op jit(solution)/shard_map/ppermute | solution.py:29
  14.0 1.2 %collective-permute-start.4 = (f32[6,8,128]{2,1,0:T(8,128)S(1)}, f32[6,8,128]{2,1,0:T(8,128)S(1)}, u32[]{:S(2)}, u32[]{:S(2)}) collective-permute-start(f32[6,8,128]{2,1,0:T(8,128)S(1)} %get-tuple-element.33), channel_id=1, source_target_pairs={{0,16},{16,0},{32,48},{48,32},{1,17},{17,1},{33,49},{49,33},{2,18}... | collective-permute-start | bytes 73736 | tf_op jit(solution)/shard_map/ppermute | solution.py:29
  15.2 7.2 %collective-permute-start.5 = (f32[6,8,128]{2,1,0:T(8,128)S(1)}, f32[6,8,128]{2,1,0:T(8,128)S(1)}, u32[]{:S(2)}, u32[]{:S(2)}) collective-permute-start(f32[6,8,128]{2,1,0:T(8,128)S(1)} %get-tuple-element.34), channel_id=1, source_target_pairs={{16,32},{32,16},{48,0},{0,48},{17,33},{33,17},{49,1},{1,49},{18,34... | collective-permute-start | bytes 73736 | tf_op jit(solution)/shard_map/ppermute | solution.py:29
  23.1 9.6 %collective-permute-start.6 = (f32[6,24,128]{2,1,0:T(8,128)S(1)}, f32[6,24,128]{2,1,0:T(8,128)S(1)}, u32[]{:S(2)}, u32[]{:S(2)}) collective-permute-start(f32[6,24,128]{2,1,0:T(8,128)S(1)} %get-tuple-element.36), channel_id=1, source_target_pairs={{0,1},{1,0},{2,3},{3,2},{4,5},{5,4},{6,7},{7,6},{8,9},{9,8},{10,11... | collective-permute-start | bytes 221192 | tf_op jit(solution)/shard_map/ppermute | solution.py:29
  24.2 8.5 %collective-permute-start.7 = (f32[6,24,128]{2,1,0:T(8,128)S(1)}, f32[6,24,128]{2,1,0:T(8,128)S(1)}, u32[]{:S(2)}, u32[]{:S(2)}) collective-permute-start(f32[6,24,128]{2,1,0:T(8,128)S(1)} %get-tuple-element.37), channel_id=1, source_target_pairs={{1,2},{2,1},{3,4},{4,3},{5,6},{6,5},{7,8},{8,7},{9,10},{10,9},{11,... | collective-permute-start | bytes 221192 | tf_op jit(solution)/shard_map/ppermute | solution.py:29
  26.2 3.7 %collective-permute-start.8 = (f32[4,8,128]{2,1,0:T(8,128)S(1)}, f32[4,8,128]{2,1,0:T(8,128)S(1)}, u32[]{:S(2)}, u32[]{:S(2)}) collective-permute-start(f32[4,8,128]{2,1,0:T(8,128)S(1)} %get-tuple-element.38), channel_id=1, source_target_pairs={{0,64},{64,0},{128,192},{192,128},{1,65},{65,1},{129,193},{193,129... | collective-permute-start | bytes 49160 | tf_op jit(solution)/shard_map/ppermute | solution.py:29
  27.7 5.0 %collective-permute-start.9 = (f32[4,8,128]{2,1,0:T(8,128)S(1)}, f32[4,8,128]{2,1,0:T(8,128)S(1)}, u32[]{:S(2)}, u32[]{:S(2)}) collective-permute-start(f32[4,8,128]{2,1,0:T(8,128)S(1)} %get-tuple-element.39), channel_id=1, source_target_pairs={{64,128},{128,64},{192,0},{0,192},{65,129},{129,65},{193,1},{1,193... | collective-permute-start | bytes 49160 | tf_op jit(solution)/shard_map/ppermute | solution.py:29
  39.9 7.1 %collective-permute-start.13 = (f32[2,8,128]{2,1,0:T(8,128)S(1)}, f32[2,8,128]{2,1,0:T(8,128)S(1)}, u32[]{:S(2)}, u32[]{:S(2)}) collective-permute-start(f32[2,8,128]{2,1,0:T(8,128)S(1)} %get-tuple-element.40.own), channel_id=1, source_target_pairs={{16,32},{32,16},{48,0},{0,48},{17,33},{33,17},{49,1},{1,49},{18,34... | collective-permute-start | bytes 24584 | tf_op jit(solution)/shard_map/ppermute | solution.py:29
  41.9 5.1 %collective-permute-start.12 = (f32[2,8,128]{2,1,0:T(8,128)S(1)}, f32[2,8,128]{2,1,0:T(8,128)S(1)}, u32[]{:S(2)}, u32[]{:S(2)}) collective-permute-start(f32[2,8,128]{2,1,0:T(8,128)S(1)} %get-tuple-element.40.own), channel_id=1, source_target_pairs={{0,16},{16,0},{32,48},{48,32},{1,17},{17,1},{33,49},{49,33},{2,18}... | collective-permute-start | bytes 24584 | tf_op jit(solution)/shard_map/ppermute | solution.py:29
  44.5 4.9 %collective-permute-start.11 = (f32[2,8,128]{2,1,0:T(8,128)S(1)}, f32[2,8,128]{2,1,0:T(8,128)S(1)}, u32[]{:S(2)}, u32[]{:S(2)}) collective-permute-start(f32[2,8,128]{2,1,0:T(8,128)S(1)} %get-tuple-element.40.own), channel_id=1, source_target_pairs={{64,128},{128,64},{192,0},{0,192},{65,129},{129,65},{193,1},{1,193... | collective-permute-start | bytes 24584 | tf_op jit(solution)/shard_map/ppermute | solution.py:29
  46.0 3.7 %collective-permute-start.10 = (f32[2,8,128]{2,1,0:T(8,128)S(1)}, f32[2,8,128]{2,1,0:T(8,128)S(1)}, u32[]{:S(2)}, u32[]{:S(2)}) collective-permute-start(f32[2,8,128]{2,1,0:T(8,128)S(1)} %get-tuple-element.40.own), channel_id=1, source_target_pairs={{0,64},{64,0},{128,192},{192,128},{1,65},{65,1},{129,193},{193,129... | collective-permute-start | bytes 24584 | tf_op jit(solution)/shard_map/ppermute | solution.py:29
  50.2 12.6 %collective-permute-start.15 = (f32[4,8,128]{2,1,0:T(8,128)S(1)}, f32[4,8,128]{2,1,0:T(8,128)S(1)}, u32[]{:S(2)}, u32[]{:S(2)}) collective-permute-start(f32[4,8,128]{2,1,0:T(8,128)S(1)} %get-tuple-element.41.vox), channel_id=1, source_target_pairs={{1,2},{2,1},{3,4},{4,3},{5,6},{6,5},{7,8},{8,7},{9,10},{10,9},{11,... | collective-permute-start | bytes 49160 | tf_op jit(solution)/shard_map/ppermute | solution.py:29
  51.5 11.3 %collective-permute-start.14 = (f32[4,8,128]{2,1,0:T(8,128)S(1)}, f32[4,8,128]{2,1,0:T(8,128)S(1)}, u32[]{:S(2)}, u32[]{:S(2)}) collective-permute-start(f32[4,8,128]{2,1,0:T(8,128)S(1)} %get-tuple-element.41.vox), channel_id=1, source_target_pairs={{0,1},{1,0},{2,3},{3,2},{4,5},{5,4},{6,7},{7,6},{8,9},{9,8},{10,11... | collective-permute-start | bytes 49160 | tf_op jit(solution)/shard_map/ppermute | solution.py:29
  57.9 4.9 %collective-permute-start.17 = (f32[2,8,128]{2,1,0:T(8,128)S(1)}, f32[2,8,128]{2,1,0:T(8,128)S(1)}, u32[]{:S(2)}, u32[]{:S(2)}) collective-permute-start(f32[2,8,128]{2,1,0:T(8,128)S(1)} %get-tuple-element.42), channel_id=1, source_target_pairs={{64,128},{128,64},{192,0},{0,192},{65,129},{129,65},{193,1},{1,193... | collective-permute-start | bytes 24584 | tf_op jit(solution)/shard_map/ppermute | solution.py:29
  59.1 3.7 %collective-permute-start.16 = (f32[2,8,128]{2,1,0:T(8,128)S(1)}, f32[2,8,128]{2,1,0:T(8,128)S(1)}, u32[]{:S(2)}, u32[]{:S(2)}) collective-permute-start(f32[2,8,128]{2,1,0:T(8,128)S(1)} %get-tuple-element.42), channel_id=1, source_target_pairs={{0,64},{64,0},{128,192},{192,128},{1,65},{65,1},{129,193},{193,129... | collective-permute-start | bytes 24584 | tf_op jit(solution)/shard_map/ppermute | solution.py:29

commit v2 on v1

--- a/solution.py
+++ b/solution.py
@@ -10,7 +10,7 @@
 
 DT = 0.1
 CHUNKS = 1
-U1, U2, U3, U4 = (5, 4, 10, 8)
+U1, U2, U3, U4 = (5, 4, 8, 8)
 F32 = jnp.float32
 VM = pl.BlockSpec(memory_space=pltpu.VMEM)
 SM = pl.BlockSpec(memory_space=pltpu.SMEM)
@@ -32,12 +32,12 @@
 PARTIAL = ()
 
 
-def call(body, outs, specs, args, scratch=(), limit=24, alias=None):
+def call(body, outs, specs, args, scratch=(), limit=24, alias=None, hbm=0):
     return pl.pallas_call(
         body,
         out_shape=[jax.ShapeDtypeStruct(s, F32) for s in outs],
         in_specs=specs,
-        out_specs=[VM] * len(outs),
+        out_specs=[HB] * hbm + [VM] * (len(outs) - hbm),
         scratch_shapes=list(scratch),
         input_output_aliases=alias or {},
         compiler_params=pltpu.CompilerParams(vmem_limit_bytes=limit << 20),
@@ -445,25 +445,66 @@
         edge[k] = value
 
 
+def stacked(parts):
+    wide_parts = [jnp.broadcast_to(q, (8, 128)) for q in parts]
+    last = jnp.where(rows((8, 128)) < 4, wide_parts[3], wide_parts[0])
+    return jnp.concatenate([wide_parts[1], wide_parts[2], last], axis=0)
+
+
+def inner_flow(d0, m0, lane):
+    fy = (d0 + up(d0, 0)) * (up(m0, 0) - m0)
+    gz = jnp.where(lane == 127, 0.0, up(m0, 1) - m0)
+    fz = (d0 + up(d0, 1)) * gz
+    return (fy - down(fy, 0)) + (fz - down(fz, 1)), gz
+
+
+def middle(vox, p, a_in, sc, sf, src):
+    n = sf.shape[0] - 2
+    for X in range(n // 8 + 2):
+        src[X] = stacked([vox[yv, X : X + 1, :] for yv in range(4)])
+
+    def scale(e, _):
+        sc[e] = a_in[e] * src[(e + 6) >> 3]
+        return 0
+
+    lax.fori_loop(0, n + 4, scale, 0, unroll=4)
+    lane = lanes((24, 128))
+
+    def third(t, f0):
+        e = t + 1
+        m0, d0 = (sc[e], p[1, e])
+        fx = (d0 + p[1, e + 1]) * (sc[e + 1] - m0)
+        flow, gz = inner_flow(d0, m0, lane)
+        sf[t] = a_in[e] * (src[(e + 6) >> 3] + 0.5 * ((fx - f0) + flow) + p[5, e] * gz)
+        return fx
+
+    lax.fori_loop(1, n + 1, third, (p[1, 1] + p[1, 2]) * (sc[2] - sc[1]), unroll=U3)
+
+
 def adjoint(
-    ends, idx, vox, rz0, rz1, re0, re1, p, t, h, a_in, later, later_z, r1, r2,
-    gd, gc, src, sc, sf, m,
+    ends, idx, vox, rz0, rz1, re0, re1, p, t, h, a_in, later, later_z, r1, r2, sc_in, sf_in,
+    gd_out, gc_out, sc, sf, gd, gc, m, sems,
 ):
     n = r2.shape[0]
     last = n // 8 + 1
     row = rows((8, 128))
-    for X in range(last + 1):
-        parts = []
-        for yv in range(4):
-            if X in (0, last) and yv in (0, 3):
-                at, k = (last - 1 if X == 0 else 1, yv // 3)
-                value = picked(ends, idx, 0, re0[k, at : at + 1, :], re1[k, at : at + 1, :])[X > 0]
-            else:
-                value = vox[yv, X : X + 1, :]
-            parts.append(jnp.broadcast_to(value, (8, 128)))
-        src[X, 0:8, :] = parts[1]
-        src[X, 8:16, :] = parts[2]
-        src[X, 16:24, :] = jnp.where(row < 4, parts[3], parts[0])
+    lane = lanes((24, 128))
+    plane = {}
+    for X in (0, last):
+        at = last - 1 if X == 0 else 1
+        parts = [vox[yv, X : X + 1, :] for yv in range(4)]
+        for k in range(2):
+            parts[3 * k] = picked(ends, idx, 0, re0[k, at : at + 1, :], re1[k, at : at + 1, :])[X > 0]
+        plane[X] = stacked(parts)
+    for X in (1, last - 1):
+        plane[X] = stacked([vox[yv, X : X + 1, :] for yv in range(4)])
+    for e in (0, 1, n + 2, n + 3):
+        sc[e] = a_in[e] * plane[(e + 6) // 8]
+    for e in (1, 2, n + 1, n + 2):
+        m0, d0 = (sc[e], p[1, e])
+        flow, gz = inner_flow(d0, m0, lane)
+        flow = flow + (d0 + p[1, e + 1]) * (sc[e + 1] - m0) - (d0 + p[1, e - 1]) * (m0 - sc[e - 1])
+        sf[e - 1] = a_in[e] * (plane[(e + 6) // 8] + 0.5 * flow + p[5, e] * gz)
 
     slot8 = lanes((8, 128)) % 4
     sources = []
@@ -480,9 +521,7 @@
                 for k in (1, 2, 4):
                     both = both + pltpu.roll(both, k, 0)
                 parts.append(both)
-            cols.append(
-                jnp.concatenate([parts[1], parts[2], jnp.where(row < 4, parts[3], parts[0])], axis=0)
-            )
+            cols.append(stacked(parts))
         sources.append(jnp.concatenate(cols, axis=1))
 
     slot = lanes((24, 256)) % 4
@@ -494,29 +533,20 @@
         (dh, ends_up(dt, dh, slot), ends_down(dt, dh, slot)), (sh, su, ends_down(st, sh, slot))
     )
     fz = ah * (sources[1] + 0.5 * flow + wide(h.at[5]) * (su - sh))
-    for k, value in enumerate((wide(h.at[0]), dh, sh, fz, wide(later_z))):
+    for k, value in enumerate((wide(h.at[0]), sh, fz, wide(later_z))):
         to_ends(m, k, value, slot)
-
-    def scale(e, _):
-        sc[e] = a_in[e] * src[(e + 6) >> 3]
+    step = jnp.where(slot == 1, up(sh, 1), down(sh, 1)) - st
+    both = dt + jnp.where(slot == 1, up(dh, 1), down(dh, 1))
+    add = at * step * (0.5 * both + jnp.where(slot == 1, wide(t.at[5]), 0.0))
+    m[4, 0] = add[:, 0:128]
+    m[4, 1] = add[:, 128:256]
+    outer = (lane == 0) | (lane == 127)
+
+    def correct(t, _):
+        sf[t] = sf[t] + jnp.where(outer, edge(m, 4, t + 1), 0.0)
         return 0
 
-    lax.fori_loop(0, n + 4, scale, 0, unroll=4)
-    lane = lanes((24, 128))
-
-    def third(t, f0):
-        e = t + 1
-        m0, d0 = (sc[e], p[1, e])
-        dh, mh = (edge(m, 1, e), edge(m, 2, e))
-        fx = (d0 + p[1, e + 1]) * (sc[e + 1] - m0)
-        fy = (d0 + up(d0, 0)) * (up(m0, 0) - m0)
-        gz = jnp.where(lane == 127, mh, up(m0, 1)) - m0
-        fz = (d0 + jnp.where(lane == 127, dh, up(d0, 1))) * gz
-        flow = (fx - f0) + (fy - down(fy, 0)) + (fz - back(fz, (d0 + dh) * (m0 - mh), lane))
-        sf[t] = a_in[e] * (src[(e + 6) >> 3] + 0.5 * flow + p[5, e] * gz)
-        return fx
-
-    lax.fori_loop(0, n + 2, third, (p[1, 0] + p[1, 1]) * (sc[1] - sc[0]), unroll=U3)
+    lax.fori_loop(0, n + 2, correct, 0, unroll=10)
     lane = lane[0:16]
 
     def fourth(x, e0):
@@ -528,7 +558,7 @@
         ex = ex + (s0 - sf[t + 1, 0:16, :]) * (p[0, e + 1, 0:16, :] - c0)
         m3, l3, s3, c3 = full
         ey = (m3 - up(m3, 0)) * (up(l3, 0) - l3) + (s3 - up(s3, 0)) * (up(c3, 0) - c3)
-        ch, mh, sh, lh = (edge(m, k, e, 16) for k in (0, 2, 3, 4))
+        ch, mh, sh, lh = (edge(m, k, e, 16) for k in range(4))
         mu, lu, su, cu = (
             jnp.where(lane == 127, b, up(a, 1)) for a, b in ((m0, mh), (l0, lh), (s0, sh), (c0, ch))
         )
@@ -540,7 +570,16 @@
 
     ex = (sc[1, 0:16, :] - sc[2, 0:16, :]) * (later[1, 0:16, :] - later[0, 0:16, :])
     ex = ex + (sf[0, 0:16, :] - sf[1, 0:16, :]) * (p[0, 2, 0:16, :] - p[0, 1, 0:16, :])
-    lax.fori_loop(0, n, fourth, ex, unroll=U4)
+    part = n // 3
+    copies = []
+    for k in range(3):
+        ex = lax.fori_loop(k * part, (k + 1) * part, fourth, ex, unroll=U4)
+        for value, out in ((gd, gd_out), (gc, gc_out)):
+            here = pl.ds(k * part, part)
+            copies.append(pltpu.make_async_copy(value.at[here], out.at[here], sems.at[len(copies)]))
+            copies[-1].start()
+    for copy in copies:
+        copy.wait()
 
 
 def coarse(x):
@@ -616,17 +655,26 @@
     rz0 = swap(vox, "gz", 0, "voxel_z0")
     re0 = swap(edge, "gx", 0, "corner_x0")
     re1 = swap(edge, "gx", 1, "corner_x1")
-    gd, gc = call(
+    sc, sf = call(
+        middle,
+        [(n + 4, 24, 128), (n + 2, 24, 128)],
+        [VM] * 3,
+        (vox, p, a),
+        [pltpu.VMEM((n // 8 + 2, 24, 128), F32)],
+    )
+    gd, gc, _, _ = call(
         partial(adjoint, ends),
-        [(n, 16, 128)] * 2,
-        [SM] + [VM] * 13,
-        (idx, vox, rz0, rz1, re0, re1, p, t, h, a, later, later_z, r1, r2),
+        [(n, 16, 128)] * 2 + [(n + 4, 24, 128), (n + 2, 24, 128)],
+        [SM] + [VM] * 15,
+        (idx, vox, rz0, rz1, re0, re1, p, t, h, a, later, later_z, r1, r2, sc, sf),
         [
-            pltpu.VMEM((n // 8 + 2, 24, 128), F32),
-            pltpu.VMEM((n + 4, 24, 128), F32),
-            pltpu.VMEM((n + 2, 24, 128), F32),
+            pltpu.VMEM((n, 16, 128), F32),
+            pltpu.VMEM((n, 16, 128), F32),
             pltpu.VMEM((5, 2, 24, 128), F32),
+            pltpu.SemaphoreType.DMA((6,)),
         ],
+        alias={14: 2, 15: 3},
+        hbm=2,
     )
     return gd, gc
 

time: 68.7 us -> 67.3 us (0.980)
  waiting for transfers between devices: 17.2 us -> 15.8 us
    ppermute x18, waiting for transfers between devices: 17.2 us -> 15.8 us  [swap(): lax.ppermute(value, axis, swap_pairs(lax.axis_size(axis), first, ends))]
    pallas_call x7 -> x8, Pallas kernels: 20 us -> 20 us  [call(): pl.pallas_call(body, out_shape=[jax.ShapeDtypeStruct(s, F32) for s in out...]
  transfers between devices with their start and end apart: 18 -> 18, of which waited for: 8 -> 8; matrix products, arithmetic and copies ran while one was open for 0% -> 0% of each run, Pallas kernels for 5% -> 7%
where the time goes in v2:
time: 67.3 us; the launch traced here: 67.1 us
  starting transfers between devices  30.5 us (45%)
  Pallas kernels  20 us (30%)
  waiting for transfers between devices  15.8 us (23%)
  between operations  0.76 us (1%)
    ppermute x18, starting transfers between devices, swap(): lax.ppermute(value, axis, swap_pairs(lax.axis_size(axis), first, ends))  30.5 us
    pallas_call x8, Pallas kernels, call(): pl.pallas_call(body, out_shape=[jax.ShapeDtypeStruct(s, F32) for s in out...  20 us
    ppermute x18, waiting for transfers between devices, swap(): lax.ppermute(value, axis, swap_pairs(lax.axis_size(axis), first, ends))  15.8 us
  transfers between devices with their start and end apart: 18, of which 8 were waited for; matrix products, arithmetic and copies ran while one was open for 0% of the time, Pallas kernels for 7%

profile of v2, /device:TPU:32, one launch (start us, length us, event | category | flops | bytes accessed | tf_op | source)
XLA Modules:
  0.0 67.1 jit_solution(10840338354581673085)
XLA Ops:
  0.6 0.0 copy-start.1
  0.7 0.1 pad_add_fusion.idx
  0.7 3.0 %shard_map.104 = (f32[6,48,16,128]{3,2,1,0:T(8,128)S(1)}, f32[10,16,128]{2,1,0:T(8,128)S(1)}, f32[10,16,128]{2,1,0:T(8,128)S(1)}, f32[60,8,128]{2,1,0:T(8,128)S(...) custom-call(s32[3]{0:T(128)S(1)} %pad_add_fusion.idx, f32[48,16,128]{2,1,0:T(8,128)} %c.1, ...), custom_call_target="tpu_custom_call" | custom-call | tf_op jit(solution)/shard_map/pallas_call | solution.py:36
  3.7 0.1 collective-permute-start.2
  3.8 6.4 %collective-permute-start.3 = (f32[60,8,128]{2,1,0:T(8,128)S(1)}, f32[60,8,128]{2,1,0:T(8,128)S(1)}, u32[]{:S(2)}, u32[]{:S(2)}) collective-permute-start(f32[60,8,128]{2,1,0:T(8,128)S(1)} %get-tuple-element.34), channel_id=1, source_target_pairs={{16,32},{32,16},{48,0},{0,48},{17,33},{33,17},{49,1},{1,49},{18,34... | collective-permute-start | bytes 737288 | tf_op jit(solution)/shard_map/ppermute | solution.py:29
  10.2 1.6 %collective-permute-start = (f32[10,16,128]{2,1,0:T(8,128)S(1)}, f32[10,16,128]{2,1,0:T(8,128)S(1)}, u32[]{:S(2)}, u32[]{:S(2)}) collective-permute-start(f32[10,16,128]{2,1,0:T(8,128)S(1)} %get-tuple-element.31), channel_id=1, source_target_pairs={{0,64},{64,0},{128,192},{192,128},{1,65},{65,1},{129,193},{193,129... | collective-permute-start | bytes 245768 | tf_op jit(solution)/shard_map/ppermute | solution.py:29
  11.8 2.2 %collective-permute-start.1 = (f32[10,16,128]{2,1,0:T(8,128)S(1)}, f32[10,16,128]{2,1,0:T(8,128)S(1)}, u32[]{:S(2)}, u32[]{:S(2)}) collective-permute-start(f32[10,16,128]{2,1,0:T(8,128)S(1)} %get-tuple-element.32), channel_id=1, source_target_pairs={{64,128},{128,64},{192,0},{0,192},{65,129},{129,65},{193,1},{1,193... | collective-permute-start | bytes 245768 | tf_op jit(solution)/shard_map/ppermute | solution.py:29
  14.0 0.0 collective-permute-start.4
  14.0 1.2 %collective-permute-done.4.ys0 = f32[6,8,128]{2,1,0:T(8,128)S(1)} collective-permute-done((f32[6,8,128]{2,1,0:T(8,128)S(1)}, f32[6,8,128]{2,1,0:T(8,128)S(1)}, u32[]{:S(2)}, u32[]{:S(2)}) %collective-permute-start.4) | collective-permute-done | bytes 24608 | tf_op jit(solution)/shard_map/ppermute | solution.py:29
  15.2 0.0 collective-permute-start.5
  15.2 1.6 %shard_map.106.tm = f32[6,2,16,128]{3,2,1,0:T(8,128)S(1)} custom-call(f32[6,48,16,128]{3,2,1,0:T(8,128)S(1)} %get-tuple-element.30.all_f), custom_call_target="tpu_custom_call" | custom-call | tf_op jit(solution)/shard_map/pallas_call | solution.py:36
  16.8 5.6 %collective-permute-done.5.ys1 = f32[6,8,128]{2,1,0:T(8,128)S(1)} collective-permute-done((f32[6,8,128]{2,1,0:T(8,128)S(1)}, f32[6,8,128]{2,1,0:T(8,128)S(1)}, u32[]{:S(2)}, u32[]{:S(2)}) %collective-permute-start.5) | collective-permute-done | bytes 24608 | tf_op jit(solution)/shard_map/ppermute | solution.py:29
  22.4 0.0 collective-permute-done.rx0
  22.4 0.0 collective-permute-done.1.rx1
  22.4 0.7 %shard_map.107 = (f32[6,2,24,128]{3,2,1,0:T(8,128)S(1)}, f32[6,24,128]{2,1,0:T(8,128)S(1)}, f32[6,24,128]{2,1,0:T(8,128)S(1)}, f32[4,8,128]{2,1,0:T(8,128)S(1)}, f32[4,8,128]{2,1,0:T(8,128)S(1)}) custom-call(s32[3]{0:T(128)S(1)} %pad_add_fusion.idx, f32[6,2,16,128]{3,2,1,0:T(8,128)S(1)} %shard_map.106.tm, f32[10,16,128]{2,1,0:T(8,128)S(1)} %collective-permute-done.rx0, ...), custom_call_target="tpu_custom_call" | custom-call | tf_op jit(solution)/shard_map/pallas_call | solution.py:36
  23.1 1.0 %collective-permute-start.6 = (f32[6,24,128]{2,1,0:T(8,128)S(1)}, f32[6,24,128]{2,1,0:T(8,128)S(1)}, u32[]{:S(2)}, u32[]{:S(2)}) collective-permute-start(f32[6,24,128]{2,1,0:T(8,128)S(1)} %get-tuple-element.40), channel_id=1, source_target_pairs={{0,1},{1,0},{2,3},{3,2},{4,5},{5,4},{6,7},{7,6},{8,9},{9,8},{10,11... | collective-permute-start | bytes 221192 | tf_op jit(solution)/shard_map/ppermute | solution.py:29
  24.2 2.0 %collective-permute-start.7 = (f32[6,24,128]{2,1,0:T(8,128)S(1)}, f32[6,24,128]{2,1,0:T(8,128)S(1)}, u32[]{:S(2)}, u32[]{:S(2)}) collective-permute-start(f32[6,24,128]{2,1,0:T(8,128)S(1)} %get-tuple-element.41), channel_id=1, source_target_pairs={{1,2},{2,1},{3,4},{4,3},{5,6},{6,5},{7,8},{8,7},{9,10},{10,9},{11,... | collective-permute-start | bytes 221192 | tf_op jit(solution)/shard_map/ppermute | solution.py:29
  26.2 1.6 %collective-permute-start.8 = (f32[4,8,128]{2,1,0:T(8,128)S(1)}, f32[4,8,128]{2,1,0:T(8,128)S(1)}, u32[]{:S(2)}, u32[]{:S(2)}) collective-permute-start(f32[4,8,128]{2,1,0:T(8,128)S(1)} %get-tuple-element.42), channel_id=1, source_target_pairs={{0,64},{64,0},{128,192},{192,128},{1,65},{65,1},{129,193},{193,129... | collective-permute-start | bytes 49160 | tf_op jit(solution)/shard_map/ppermute | solution.py:29
  27.7 0.0 collective-permute-done.2.ry0
  27.7 0.7 %collective-permute-start.9 = (f32[4,8,128]{2,1,0:T(8,128)S(1)}, f32[4,8,128]{2,1,0:T(8,128)S(1)}, u32[]{:S(2)}, u32[]{:S(2)}) collective-permute-start(f32[4,8,128]{2,1,0:T(8,128)S(1)} %get-tuple-element.43), channel_id=1, source_target_pairs={{64,128},{128,64},{192,0},{0,192},{65,129},{129,65},{193,1},{1,193... | collective-permute-start | bytes 49160 | tf_op jit(solution)/shard_map/ppermute | solution.py:29
  28.5 0.0 copy-done.1
  28.5 0.0 copy-done.2
  28.5 0.0 collective-permute-done.3.ry1
  28.5 1.1 %shard_map.105 = (f32[6,52,24,128]{3,2,1,0:T(8,128)S(1)}, f32[52,24,128]{2,1,0:T(8,128)S(1)}) custom-call(s32[3]{0:T(128)S(1)} %pad_add_fusion.idx, f32[6,48,16,128]{3,2,1,0:T(8,128)S(1)} %get-tuple-element.30.all_f, f32[10,16,128]{2,1,0:T(8,128)S(1)} %collective-permute-done.rx0, f32[10,16,128]{2,1,0:T(8,128)S(1)} %collective-permute-done.1.rx1, ...), custom_call_target="tpu_custom_call" | custom-call | tf_op jit(solution)/shard_map/pallas_call | solution.py:36
  29.6 0.3 collective-permute-done.8.re0
  29.9 2.8 %collective-permute-done.9.re1 = f32[4,8,128]{2,1,0:T(8,128)S(1)} collective-permute-done((f32[4,8,128]{2,1,0:T(8,128)S(1)}, f32[4,8,128]{2,1,0:T(8,128)S(1)}, u32[]{:S(2)}, u32[]{:S(2)}) %collective-permute-start.9) | collective-permute-done | bytes 16416 | tf_op jit(solution)/shard_map/ppermute | solution.py:29
  32.7 0.0 collective-permute-done.6.rz0
  32.7 0.0 collective-permute-done.7.rz1
  32.7 7.2 %shard_map.108 = (f32[6,52,24,128]{3,2,1,0:T(8,128)S(1)}, f32[2,8,128]{2,1,0:T(8,128)S(1)}, f32[6,2,24,128]{3,2,1,0:T(8,128)S(1)}, f32[52,24,128]{2,1,0:T(8,128)...) custom-call(s32[3]{0:T(128)S(1)} %pad_add_fusion.idx, ...), custom_call_target="tpu_custom_call", output_to_operand_aliasing={{0}: (2, {}), {3}: (3, {})} | custom-call | tf_op jit(solution)/shard_map/pallas_call | solution.py:36
  40.0 2.0 %collective-permute-start.13 = (f32[2,8,128]{2,1,0:T(8,128)S(1)}, f32[2,8,128]{2,1,0:T(8,128)S(1)}, u32[]{:S(2)}, u32[]{:S(2)}) collective-permute-start(f32[2,8,128]{2,1,0:T(8,128)S(1)} %get-tuple-element.44.own), channel_id=1, source_target_pairs={{16,32},{32,16},{48,0},{0,48},{17,33},{33,17},{49,1},{1,49},{18,34... | collective-permute-start | bytes 24584 | tf_op jit(solution)/shard_map/ppermute | solution.py:29
  42.0 2.5 %collective-permute-start.12 = (f32[2,8,128]{2,1,0:T(8,128)S(1)}, f32[2,8,128]{2,1,0:T(8,128)S(1)}, u32[]{:S(2)}, u32[]{:S(2)}) collective-permute-start(f32[2,8,128]{2,1,0:T(8,128)S(1)} %get-tuple-element.44.own), channel_id=1, source_target_pairs={{0,16},{16,0},{32,48},{48,32},{1,17},{17,1},{33,49},{49,33},{2,18}... | collective-permute-start | bytes 24584 | tf_op jit(solution)/shard_map/ppermute | solution.py:29
  44.5 1.5 %collective-permute-start.11 = (f32[2,8,128]{2,1,0:T(8,128)S(1)}, f32[2,8,128]{2,1,0:T(8,128)S(1)}, u32[]{:S(2)}, u32[]{:S(2)}) collective-permute-start(f32[2,8,128]{2,1,0:T(8,128)S(1)} %get-tuple-element.44.own), channel_id=1, source_target_pairs={{64,128},{128,64},{192,0},{0,192},{65,129},{129,65},{193,1},{1,193... | collective-permute-start | bytes 24584 | tf_op jit(solution)/shard_map/ppermute | solution.py:29
  46.0 0.0 collective-permute-start.10
  46.0 1.0 %collective-permute-done.13.ry1 = f32[2,8,128]{2,1,0:T(8,128)S(1)} collective-permute-done((f32[2,8,128]{2,1,0:T(8,128)S(1)}, f32[2,8,128]{2,1,0:T(8,128)S(1)}, u32[]{:S(2)}, u32[]{:S(2)}) %collective-permute-start.13) | collective-permute-done | bytes 8224 | tf_op jit(solution)/shard_map/ppermute | solution.py:29
  47.0 0.0 collective-permute-done.12.ry0
  47.0 2.3 %collective-permute-done.11.rx1 = f32[2,8,128]{2,1,0:T(8,128)S(1)} collective-permute-done((f32[2,8,128]{2,1,0:T(8,128)S(1)}, f32[2,8,128]{2,1,0:T(8,128)S(1)}, u32[]{:S(2)}, u32[]{:S(2)}) %collective-permute-start.11) | collective-permute-done | bytes 8224 | tf_op jit(solution)/shard_map/ppermute | solution.py:29
  49.4 0.3 collective-permute-done.10.rx0
  49.7 0.6 shard_map.109
  50.2 1.3 %collective-permute-start.15 = (f32[4,8,128]{2,1,0:T(8,128)S(1)}, f32[4,8,128]{2,1,0:T(8,128)S(1)}, u32[]{:S(2)}, u32[]{:S(2)}) collective-permute-start(f32[4,8,128]{2,1,0:T(8,128)S(1)} %get-tuple-element.45.vox), channel_id=1, source_target_pairs={{1,2},{2,1},{3,4},{4,3},{5,6},{6,5},{7,8},{8,7},{9,10},{10,9},{11,... | collective-permute-start | bytes 49160 | tf_op jit(solution)/shard_map/ppermute | solution.py:29
  51.5 6.4 %collective-permute-start.14 = (f32[4,8,128]{2,1,0:T(8,128)S(1)}, f32[4,8,128]{2,1,0:T(8,128)S(1)}, u32[]{:S(2)}, u32[]{:S(2)}) collective-permute-start(f32[4,8,128]{2,1,0:T(8,128)S(1)} %get-tuple-element.45.vox), channel_id=1, source_target_pairs={{0,1},{1,0},{2,3},{3,2},{4,5},{5,4},{6,7},{7,6},{8,9},{9,8},{10,11... | collective-permute-start | bytes 49160 | tf_op jit(solution)/shard_map/ppermute | solution.py:29
  57.9 1.2 %collective-permute-start.17 = (f32[2,8,128]{2,1,0:T(8,128)S(1)}, f32[2,8,128]{2,1,0:T(8,128)S(1)}, u32[]{:S(2)}, u32[]{:S(2)}) collective-permute-start(f32[2,8,128]{2,1,0:T(8,128)S(1)} %get-tuple-element.46), channel_id=1, source_target_pairs={{64,128},{128,64},{192,0},{0,192},{65,129},{129,65},{193,1},{1,193... | collective-permute-start | bytes 24584 | tf_op jit(solution)/shard_map/ppermute | solution.py:29
  59.1 0.0 collective-permute-start.16
  59.1 1.4 %shard_map.110 = (f32[52,24,128]{2,1,0:T(8,128)S(1)}, f32[50,24,128]{2,1,0:T(8,128)S(1)}) custom-call(f32[4,8,128]{2,1,0:T(8,128)S(1)} %get-tuple-element.45.vox, f32[6,52,24,128]{3,2,1,0:T(8,128)S(1)} %get-tuple-element.47.p, f32[52,24,128]{2,1,0:T(8,128)S(1)} %get-tuple-element.49.a_in), custom_call_target="tpu_custom_call" | custom-call | tf_op jit(solution)/shard_map/pallas_call | solution.py:36
  60.6 2.2 %collective-permute-done.17.re1 = f32[2,8,128]{2,1,0:T(8,128)S(1)} collective-permute-done((f32[2,8,128]{2,1,0:T(8,128)S(1)}, f32[2,8,128]{2,1,0:T(8,128)S(1)}, u32[]{:S(2)}, u32[]{:S(2)}) %collective-permute-start.17) | collective-permute-done | bytes 8224 | tf_op jit(solution)/shard_map/ppermute | solution.py:29
  62.8 0.0 collective-permute-done.16.re0
  62.8 0.0 collective-permute-done.15.rz1
  62.8 0.0 collective-permute-done.14.rz0
  62.8 4.3 %shard_map.111 = (f32[48,16,128]{2,1,0:T(8,128)}, f32[48,16,128]{2,1,0:T(8,128)}, f32[52,24,128]{2,1,0:T(8,128)S(1)}, f32[50,24,128]{2,1,0:T(8,128)S(1)}) custom-call(s32[3]{0:T(128)S(1)} %pad_add_fusion.idx, f32[4,8,128]{2,1,0:T(8,128)S(1)} %get-tuple-element.45.vox, ...), custom_call_target="tpu_custom_call", output_to_operand_aliasing={{2}: (14, {}), {3}: (15, {})} | custom-call | tf_op jit(solution)/shard_map/pallas_call | solution.py:36
  (7 shorter events, 0.0 us)
Async XLA Ops:
  0.6 27.8 %copy-start.1 = (s32[6,2,16]{2,1,0:T(2,128)S(1)}, s32[6,2,16]{2,1,0:T(2,128)}, u32[]{:S(2)}) copy-start(s32[6,2,16]{2,1,0:T(2,128)} %param.15) | copy-start | bytes 2308
  0.6 27.8 %copy-start.2 = (s32[6,2,16]{2,1,0:T(2,128)S(1)}, s32[6,2,16]{2,1,0:T(2,128)}, u32[]{:S(2)}) copy-start(s32[6,2,16]{2,1,0:T(2,128)} %param.16) | copy-start | bytes 2308
  0.7 32.0 %copy-start = (f32[4]{0:T(128)S(1)}, f32[4]{0:T(128)}, u32[]{:S(2)}) copy-start(f32[4]{0:T(128)} %cw.1) | copy-start | bytes 52
  3.7 24.0 %collective-permute-start.2 = (f32[60,8,128]{2,1,0:T(8,128)S(1)}, f32[60,8,128]{2,1,0:T(8,128)S(1)}, u32[]{:S(2)}, u32[]{:S(2)}) collective-permute-start(f32[60,8,128]{2,1,0:T(8,128)S(1)} %get-tuple-element.33), channel_id=1, source_target_pairs={{0,16},{16,0},{32,48},{48,32},{1,17},{17,1},{33,49},{49,33},{2,18}... | collective-permute-start | bytes 737288 | tf_op jit(solution)/shard_map/ppermute | solution.py:29
  3.8 24.7 %collective-permute-start.3 = (f32[60,8,128]{2,1,0:T(8,128)S(1)}, f32[60,8,128]{2,1,0:T(8,128)S(1)}, u32[]{:S(2)}, u32[]{:S(2)}) collective-permute-start(f32[60,8,128]{2,1,0:T(8,128)S(1)} %get-tuple-element.34), channel_id=1, source_target_pairs={{16,32},{32,16},{48,0},{0,48},{17,33},{33,17},{49,1},{1,49},{18,34... | collective-permute-start | bytes 737288 | tf_op jit(solution)/shard_map/ppermute | solution.py:29
  10.2 12.2 %collective-permute-start = (f32[10,16,128]{2,1,0:T(8,128)S(1)}, f32[10,16,128]{2,1,0:T(8,128)S(1)}, u32[]{:S(2)}, u32[]{:S(2)}) collective-permute-start(f32[10,16,128]{2,1,0:T(8,128)S(1)} %get-tuple-element.31), channel_id=1, source_target_pairs={{0,64},{64,0},{128,192},{192,128},{1,65},{65,1},{129,193},{193,129... | collective-permute-start | bytes 245768 | tf_op jit(solution)/shard_map/ppermute | solution.py:29
  11.8 10.6 %collective-permute-start.1 = (f32[10,16,128]{2,1,0:T(8,128)S(1)}, f32[10,16,128]{2,1,0:T(8,128)S(1)}, u32[]{:S(2)}, u32[]{:S(2)}) collective-permute-start(f32[10,16,128]{2,1,0:T(8,128)S(1)} %get-tuple-element.32), channel_id=1, source_target_pairs={{64,128},{128,64},{192,0},{0,192},{65,129},{129,65},{193,1},{1,193... | collective-permute-start | bytes 245768 | tf_op jit(solution)/shard_map/ppermute | solution.py:29
  14.0 1.2 %collective-permute-start.4 = (f32[6,8,128]{2,1,0:T(8,128)S(1)}, f32[6,8,128]{2,1,0:T(8,128)S(1)}, u32[]{:S(2)}, u32[]{:S(2)}) collective-permute-start(f32[6,8,128]{2,1,0:T(8,128)S(1)} %get-tuple-element.37), channel_id=1, source_target_pairs={{0,16},{16,0},{32,48},{48,32},{1,17},{17,1},{33,49},{49,33},{2,18}... | collective-permute-start | bytes 73736 | tf_op jit(solution)/shard_map/ppermute | solution.py:29
  15.2 7.2 %collective-permute-start.5 = (f32[6,8,128]{2,1,0:T(8,128)S(1)}, f32[6,8,128]{2,1,0:T(8,128)S(1)}, u32[]{:S(2)}, u32[]{:S(2)}) collective-permute-start(f32[6,8,128]{2,1,0:T(8,128)S(1)} %get-tuple-element.38), channel_id=1, source_target_pairs={{16,32},{32,16},{48,0},{0,48},{17,33},{33,17},{49,1},{1,49},{18,34... | collective-permute-start | bytes 73736 | tf_op jit(solution)/shard_map/ppermute | solution.py:29
  23.1 9.6 %collective-permute-start.6 = (f32[6,24,128]{2,1,0:T(8,128)S(1)}, f32[6,24,128]{2,1,0:T(8,128)S(1)}, u32[]{:S(2)}, u32[]{:S(2)}) collective-permute-start(f32[6,24,128]{2,1,0:T(8,128)S(1)} %get-tuple-element.40), channel_id=1, source_target_pairs={{0,1},{1,0},{2,3},{3,2},{4,5},{5,4},{6,7},{7,6},{8,9},{9,8},{10,11... | collective-permute-start | bytes 221192 | tf_op jit(solution)/shard_map/ppermute | solution.py:29
  24.2 8.5 %collective-permute-start.7 = (f32[6,24,128]{2,1,0:T(8,128)S(1)}, f32[6,24,128]{2,1,0:T(8,128)S(1)}, u32[]{:S(2)}, u32[]{:S(2)}) collective-permute-start(f32[6,24,128]{2,1,0:T(8,128)S(1)} %get-tuple-element.41), channel_id=1, source_target_pairs={{1,2},{2,1},{3,4},{4,3},{5,6},{6,5},{7,8},{8,7},{9,10},{10,9},{11,... | collective-permute-start | bytes 221192 | tf_op jit(solution)/shard_map/ppermute | solution.py:29
  26.2 3.7 %collective-permute-start.8 = (f32[4,8,128]{2,1,0:T(8,128)S(1)}, f32[4,8,128]{2,1,0:T(8,128)S(1)}, u32[]{:S(2)}, u32[]{:S(2)}) collective-permute-start(f32[4,8,128]{2,1,0:T(8,128)S(1)} %get-tuple-element.42), channel_id=1, source_target_pairs={{0,64},{64,0},{128,192},{192,128},{1,65},{65,1},{129,193},{193,129... | collective-permute-start | bytes 49160 | tf_op jit(solution)/shard_map/ppermute | solution.py:29
  27.7 5.0 %collective-permute-start.9 = (f32[4,8,128]{2,1,0:T(8,128)S(1)}, f32[4,8,128]{2,1,0:T(8,128)S(1)}, u32[]{:S(2)}, u32[]{:S(2)}) collective-permute-start(f32[4,8,128]{2,1,0:T(8,128)S(1)} %get-tuple-element.43), channel_id=1, source_target_pairs={{64,128},{128,64},{192,0},{0,192},{65,129},{129,65},{193,1},{1,193... | collective-permute-start | bytes 49160 | tf_op jit(solution)/shard_map/ppermute | solution.py:29
  40.0 7.1 %collective-permute-start.13 = (f32[2,8,128]{2,1,0:T(8,128)S(1)}, f32[2,8,128]{2,1,0:T(8,128)S(1)}, u32[]{:S(2)}, u32[]{:S(2)}) collective-permute-start(f32[2,8,128]{2,1,0:T(8,128)S(1)} %get-tuple-element.44.own), channel_id=1, source_target_pairs={{16,32},{32,16},{48,0},{0,48},{17,33},{33,17},{49,1},{1,49},{18,34... | collective-permute-start | bytes 24584 | tf_op jit(solution)/shard_map/ppermute | solution.py:29
  42.0 5.1 %collective-permute-start.12 = (f32[2,8,128]{2,1,0:T(8,128)S(1)}, f32[2,8,128]{2,1,0:T(8,128)S(1)}, u32[]{:S(2)}, u32[]{:S(2)}) collective-permute-start(f32[2,8,128]{2,1,0:T(8,128)S(1)} %get-tuple-element.44.own), channel_id=1, source_target_pairs={{0,16},{16,0},{32,48},{48,32},{1,17},{17,1},{33,49},{49,33},{2,18}... | collective-permute-start | bytes 24584 | tf_op jit(solution)/shard_map/ppermute | solution.py:29
  44.5 4.9 %collective-permute-start.11 = (f32[2,8,128]{2,1,0:T(8,128)S(1)}, f32[2,8,128]{2,1,0:T(8,128)S(1)}, u32[]{:S(2)}, u32[]{:S(2)}) collective-permute-start(f32[2,8,128]{2,1,0:T(8,128)S(1)} %get-tuple-element.44.own), channel_id=1, source_target_pairs={{64,128},{128,64},{192,0},{0,192},{65,129},{129,65},{193,1},{1,193... | collective-permute-start | bytes 24584 | tf_op jit(solution)/shard_map/ppermute | solution.py:29
  46.0 3.7 %collective-permute-start.10 = (f32[2,8,128]{2,1,0:T(8,128)S(1)}, f32[2,8,128]{2,1,0:T(8,128)S(1)}, u32[]{:S(2)}, u32[]{:S(2)}) collective-permute-start(f32[2,8,128]{2,1,0:T(8,128)S(1)} %get-tuple-element.44.own), channel_id=1, source_target_pairs={{0,64},{64,0},{128,192},{192,128},{1,65},{65,1},{129,193},{193,129... | collective-permute-start | bytes 24584 | tf_op jit(solution)/shard_map/ppermute | solution.py:29
  50.2 12.6 %collective-permute-start.15 = (f32[4,8,128]{2,1,0:T(8,128)S(1)}, f32[4,8,128]{2,1,0:T(8,128)S(1)}, u32[]{:S(2)}, u32[]{:S(2)}) collective-permute-start(f32[4,8,128]{2,1,0:T(8,128)S(1)} %get-tuple-element.45.vox), channel_id=1, source_target_pairs={{1,2},{2,1},{3,4},{4,3},{5,6},{6,5},{7,8},{8,7},{9,10},{10,9},{11,... | collective-permute-start | bytes 49160 | tf_op jit(solution)/shard_map/ppermute | solution.py:29
  51.5 11.3 %collective-permute-start.14 = (f32[4,8,128]{2,1,0:T(8,128)S(1)}, f32[4,8,128]{2,1,0:T(8,128)S(1)}, u32[]{:S(2)}, u32[]{:S(2)}) collective-permute-start(f32[4,8,128]{2,1,0:T(8,128)S(1)} %get-tuple-element.45.vox), channel_id=1, source_target_pairs={{0,1},{1,0},{2,3},{3,2},{4,5},{5,4},{6,7},{7,6},{8,9},{9,8},{10,11... | collective-permute-start | bytes 49160 | tf_op jit(solution)/shard_map/ppermute | solution.py:29
  57.9 4.9 %collective-permute-start.17 = (f32[2,8,128]{2,1,0:T(8,128)S(1)}, f32[2,8,128]{2,1,0:T(8,128)S(1)}, u32[]{:S(2)}, u32[]{:S(2)}) collective-permute-start(f32[2,8,128]{2,1,0:T(8,128)S(1)} %get-tuple-element.46), channel_id=1, source_target_pairs={{64,128},{128,64},{192,0},{0,192},{65,129},{129,65},{193,1},{1,193... | collective-permute-start | bytes 24584 | tf_op jit(solution)/shard_map/ppermute | solution.py:29
  59.1 3.7 %collective-permute-start.16 = (f32[2,8,128]{2,1,0:T(8,128)S(1)}, f32[2,8,128]{2,1,0:T(8,128)S(1)}, u32[]{:S(2)}, u32[]{:S(2)}) collective-permute-start(f32[2,8,128]{2,1,0:T(8,128)S(1)} %get-tuple-element.46), channel_id=1, source_target_pairs={{0,64},{64,0},{128,192},{192,128},{1,65},{65,1},{129,193},{193,129... | collective-permute-start | bytes 24584 | tf_op jit(solution)/shard_map/ppermute | solution.py:29
